TPU v7x, 256 devices: a whole 4x4x8 slice. The times are simulated.
256 devices in a mesh: head: 4 (over x), blk: 64 (over y, z, core).
Axes of the slice: x: 4, y: 4, z: 8, core: 2. Of those that a mesh axis runs over, the one named last changes fastest.
Arguments:
- hidden_in: bfloat16 [16384, 1536], P('blk'), may hold values from -6 to 6
- attn_gain: float32 [1536], replicated, may hold values from 0.5 to 2
- w_query: bfloat16 [1536, 1536], P(None, 'head'), may hold values from -0.15625 to 0.15625
- w_keyval: bfloat16 [2, 1536, 256], replicated, may hold values from -0.375 to 0.375
- prefix_cache: bfloat16 [4096, 2, 256], P('blk'), may hold values from -490 to 490
- w_out: bfloat16 [1536, 1536], P('head'), may hold values from -0.15625 to 0.15625
- moe_gain: float32 [1536], replicated, may hold values from 0.5 to 2
- w_gateup: bfloat16 [64, 1536, 768], P('blk'), may hold values from -0.15625 to 0.15625
- w_down: bfloat16 [64, 384, 1536], P('blk'), may hold values from -0.21875 to 0.21875
- routes: int32 [16384, 4], P('blk'), may hold values from 0 to 31, all different within a row; in each aligned block of 64 rows (0 to 63, 64 to 127, ...) at most 16 rows name the same one
- route_weights: float32 [16384, 4], P('blk'), may hold values from 0.1 to 1
- lengths: int32 [32], replicated, may hold values from 1 to 2048, 16384 in all
Outputs:
- layer_out: bfloat16 [16384, 1536], P('blk', 'head')
Inputs may be any that keep to these rules, and one draw needn't show every extreme that they name: The lengths sum to 16384; the longest is exactly 2048. `routes`: each row names 4 different experts. In each aligned block of 64 rows no expert is named by more than 16 rows, a bound that some block reaches.
All inputs are finite; a program needn't handle non-finite values.
Results may differ from a plain program's by a relative error of at most 0.02.
The roundings to bfloat16 on the way count: a program that leaves them out, or rounds other values in their place, can miss the bound.
Values may be sent and summed in bfloat16 or wider, within the bound.
A program may use at most 128 MiB of HBM per device.

v0:
```python
import jax
import jax.numpy as jnp
from jax import lax
from jax.sharding import PartitionSpec as P

KVH = 2
HD = 128
TOPK = 4


def passed_along(value, axis, by):
    devices = lax.axis_size(axis)
    pairs = [(i, i + by) for i in range(devices) if 0 <= i + by < devices]
    return lax.ppermute(value, axis, pairs)


def rms_norm(values, gain):
    wide = values.astype(jnp.float32)
    return wide * lax.rsqrt(jnp.mean(wide * wide, axis=-1, keepdims=True) + 1e-05) * gain


def rotate(vectors, positions):
    half = vectors.shape[-1] // 2
    freqs = 10000.0 ** (-2.0 * jnp.arange(half, dtype=jnp.float32) / vectors.shape[-1])
    angle = positions[:, None] * freqs[None, :]
    cosine = jnp.cos(angle)[:, None, :]
    sine = jnp.sin(angle)[:, None, :]
    first = vectors[..., :half]
    second = vectors[..., half:]
    return jnp.concatenate(
        [first * cosine - second * sine, second * cosine + first * sine], axis=-1
    )


def request_info(index, lengths):
    ends = jnp.cumsum(lengths)
    seg = jnp.sum((index[:, None] >= ends[None, :]).astype(jnp.int32), axis=1)
    starts = ends - lengths
    count = lengths.shape[0]
    begin = jnp.sum(
        jnp.where(seg[:, None] == jnp.arange(count, dtype=jnp.int32)[None, :], starts[None, :], 0),
        axis=1,
    )
    return (seg, index - begin)


def matmul(left, right):
    return jnp.dot(left, right, preferred_element_type=jnp.float32)


def attend(state, queries, piece, valid):
    best, total, accum = state
    keys = piece[:, :HD]
    values = piece[:, HD:]
    scores = lax.dot_general(
        queries, keys, (((1,), (1,)), ((), ())), preferred_element_type=jnp.float32
    )
    if valid is not None:
        scores = jnp.where(valid, scores, -1e30)
    new_best = jnp.maximum(best, jnp.max(scores, axis=1))
    weights = jnp.exp(scores - new_best[:, None])
    if valid is not None:
        weights = jnp.where(valid, weights, 0.0)
    rescale = jnp.exp(best - new_best)
    total = total * rescale + jnp.sum(weights, axis=1)
    accum = accum * rescale[:, None] + matmul(weights.astype(jnp.bfloat16), values)
    return (new_best, total, accum)


def attend_blocks(state, queries, piece, key_start, masker):
    count = piece.shape[0]
    width = 2048 if count > 2048 and count % 2048 == 0 else count

    def one_part(number, current):
        part = lax.dynamic_slice_in_dim(piece, number * width, width, 0)
        valid = masker(key_start + number * width, width) if masker is not None else None
        return attend(current, queries, part, valid)

    if width == count:
        return one_part(0, state)
    return lax.fori_loop(0, count // width, one_part, state)


def shards(
    hidden_in,
    attn_gain,
    w_query,
    w_keyval,
    prefix_cache,
    w_out,
    moe_gain,
    w_gateup,
    w_down,
    routes,
    route_weights,
    lengths,
):
    tok_rows = hidden_in.shape[0]
    head_index = lax.axis_index("head")
    block_index = lax.axis_index("blk")
    head_count = lax.axis_size("head")
    block_count = lax.axis_size("blk")
    local_heads = w_query.shape[1] // HD
    kv_head = head_index // (head_count // KVH)
    prefix_total = prefix_cache.shape[0] * block_count
    normed = rms_norm(hidden_in, attn_gain).astype(jnp.bfloat16)
    token_index = block_index * tok_rows + jnp.arange(tok_rows, dtype=jnp.int32)
    seg_query, offset_query = request_info(token_index, lengths)
    positions = (prefix_total + offset_query).astype(jnp.float32)
    queries = matmul(normed, w_query).reshape(tok_rows, local_heads, HD)
    queries = (
        (rotate(queries, positions) * HD ** (-0.5))
        .astype(jnp.bfloat16)
        .reshape(tok_rows * local_heads, HD)
    )
    own_weights = lax.dynamic_index_in_dim(w_keyval, kv_head, 0, keepdims=False)
    keyval = matmul(normed, own_weights)
    new_keys = rotate(keyval[:, None, :HD], positions)[:, 0, :]
    own_block = jnp.concatenate([new_keys, keyval[:, HD:]], axis=1).astype(jnp.bfloat16)
    cached = lax.dynamic_index_in_dim(prefix_cache, kv_head, 1, keepdims=False)
    row_index = jnp.repeat(token_index, local_heads)
    row_seg = jnp.repeat(seg_query, local_heads)
    row_total = tok_rows * local_heads

    def suffix_mask(key_start, count):
        key_index = key_start + jnp.arange(count, dtype=jnp.int32)
        key_seg, unused = request_info(key_index, lengths)
        return (
            (row_seg[:, None] == key_seg[None, :])
            & (key_index[None, :] <= row_index[:, None])
            & (key_index[None, :] >= 0)
        )

    state = (
        jnp.full((row_total,), -1e30, jnp.float32),
        jnp.zeros((row_total,), jnp.float32),
        jnp.zeros((row_total, HD), jnp.float32),
    )
    state = attend_blocks(
        state, queries, lax.all_gather(cached, "blk", axis=0, tiled=True), jnp.int32(0), None
    )
    state = attend_blocks(state, queries, own_block, block_index * tok_rows, suffix_mask)
    travelling = own_block
    reach = min(8, block_count // 2)
    for distance in range(reach):
        travelling = passed_along(travelling, "blk", 1)
        state = attend_blocks(
            state, queries, travelling, (block_index - distance - 1) * tok_rows, suffix_mask
        )
    best, total, accum = state
    context = (accum / total[:, None]).astype(jnp.bfloat16).reshape(tok_rows, local_heads * HD)
    quarter = tok_rows // head_count
    attn_share = lax.psum_scatter(
        matmul(context, w_out).astype(jnp.bfloat16), "head", scatter_dimension=0, tiled=True
    ).astype(jnp.float32)
    resid = lax.dynamic_slice_in_dim(hidden_in, head_index * quarter, quarter, 0)
    middle = (resid.astype(jnp.float32) + attn_share).astype(jnp.bfloat16)
    moe_in = rms_norm(middle, moe_gain).astype(jnp.bfloat16)
    my_routes = lax.dynamic_slice_in_dim(routes, head_index * quarter, quarter, 0)
    my_weights = lax.dynamic_slice_in_dim(route_weights, head_index * quarter, quarter, 0)
    expert_count = block_count // 2
    capacity = max(2, min(2 * quarter * TOPK // expert_count, quarter))
    width_d = moe_in.shape[1]
    flat_ids = my_routes.reshape(-1)
    onehot = (flat_ids[:, None] == jnp.arange(expert_count, dtype=jnp.int32)[None, :]).astype(
        jnp.int32
    )
    slots = jnp.sum((jnp.cumsum(onehot, axis=0) - 1) * onehot, axis=1)
    target = flat_ids * capacity + slots
    table = (
        target[:, None] == jnp.arange(expert_count * capacity, dtype=jnp.int32)[None, :]
    ).astype(jnp.bfloat16)
    repeated = jnp.repeat(moe_in, TOPK, axis=0)
    packed = lax.dot_general(
        table, repeated, (((0,), (0,)), ((), ())), preferred_element_type=jnp.float32
    ).astype(jnp.bfloat16)
    gate_up = w_gateup[0]
    down = w_down[0]
    half_units = down.shape[0]
    doubled = jnp.broadcast_to(
        packed.reshape(expert_count, 1, capacity, width_d), (expert_count, 2, capacity, width_d)
    )
    outgoing = doubled.reshape(2 * expert_count, capacity, width_d)
    received = lax.all_to_all(outgoing, "blk", split_axis=0, concat_axis=0, tiled=True)
    senders, count, depth = received.shape
    rows = received.reshape(senders * count, depth)
    both = matmul(rows, gate_up)
    hidden = (jax.nn.relu(both[:, :half_units]) * both[:, half_units:]).astype(jnp.bfloat16)
    partial_value = matmul(hidden, down).reshape(senders, count, depth)
    back = lax.all_to_all(
        partial_value.astype(jnp.bfloat16), "blk", split_axis=0, concat_axis=0, tiled=True
    ).astype(partial_value.dtype)
    outputs = (
        jnp.sum(back.reshape(expert_count, 2, capacity, width_d), axis=1)
        .astype(jnp.bfloat16)
        .reshape(expert_count * capacity, width_d)
    )
    picked = outputs[target].astype(jnp.float32).reshape(quarter, TOPK, width_d)
    mixed = jnp.sum(picked * my_weights[:, :, None], axis=1)
    final = (middle.astype(jnp.float32) + mixed).astype(jnp.bfloat16)
    return lax.all_to_all(final, "head", split_axis=1, concat_axis=0, tiled=True)


def solution(mesh):
    return jax.shard_map(
        shards,
        mesh=mesh,
        in_specs=(
            P("blk", None),
            P(),
            P(None, "head"),
            P(),
            P("blk", None, None),
            P("head", None),
            P(),
            P("blk", None, None),
            P("blk", None, None),
            P("blk", None),
            P("blk", None),
            P(),
        ),
        out_specs=P("blk", "head"),
        check_vma=False,
    )
```

profile of v0, /device:TPU:32, one launch (start us, length us, event | category | flops | bytes accessed | tf_op | source)
XLA Modules:
  0.0 343.7 jit_solution(14942719178354334393)
XLA Ops:
  9.7 2.0 fusion.30
  14.8 1.9 collective-permute-start
  17.7 1.9 fusion.85
  22.6 2.1 fusion.135
  24.7 3.9 %collective-permute-start.1 = (bf16[256,256]{0,1:T(8,128)(2,1)}, bf16[256,256]{0,1:T(8,128)(2,1)S(1)}, u32[]{:S(2)}, u32[]{:S(2)}) collective-permute-start(bf16[256,256]{0,1:T(8,128)(2,1)} %collective-permute-done), channel_id=1, source_target_pairs={{0,1},{1,2},{2,3},{3,4},{4,5},{5,6},{6,7},{7,8},{8,9},{9,10},{10,1... | collective-permute-start | bytes 393224 | tf_op jit(solution)/shard_map/ppermute | solution.py:14
  28.7 2.1 fusion.134
  31.2 1.9 collective-permute-start.2
  34.4 3.2 collective-permute-done.2
  40.8 3.2 collective-permute-done.3
  47.3 3.1 collective-permute-done.4
  53.5 3.1 collective-permute-done.5
  56.6 1.9 collective-permute-start.6
  59.9 3.5 %collective-permute-done.6 = bf16[256,256]{0,1:T(8,128)(2,1)S(1)} collective-permute-done((bf16[256,256]{0,1:T(8,128)(2,1)S(1)}, bf16[256,256]{0,1:T(8,128)(2,1)S(1)}, u32[]{:S(2)}, u32[]{:S(2)}) %collective-permute-start.6) | collective-permute-done | bytes 131104 | tf_op jit(solution)/shard_map/ppermute | solution.py:14
  66.6 3.4 collective-permute-done.7
  71.9 17.5 %all-gather.3.cloned.1.call-done = bf16[4096,1,256]{2,0,1:T(8,128)(2,1)} async-done(((bf16[64,1,256]{2,0,1:T(8,128)(2,1)}), bf16[4096,1,256]{2,0,1:T(8,128)(2,1)}) %all-gather.3.cloned.1.call-update) | async-done | bytes 2097168 | tf_op jit(solution)/shard_map/all_gather | solution.py:140
  89.3 10.6 %while.18 = (s32[]{:T(128)}, f32[768]{0:T(1024)S(1)}, f32[768]{0:T(1024)S(1)}, f32[768,128]{1,0:T(8,128)S(1)}, bf16[4096,256]{1,0:T(8,128)(2,1)}, /*index=5*/bf1...) while((s32[]{:T(128)}, f32[768]{0:T(1024)S(1)}, ...), condition=%wide.region_7.8_spmd.clone, body=%wide.region_4.7_spmd.clone.sunk | while | flops 813469440 | bytes 20955336 | solution.py:81
  89.3 2.0 fusion.163
  92.3 2.3 fusion.166
  94.6 2.0 fusion.163
  97.6 2.3 fusion.166
  100.0 2.5 fusion.33
  113.8 2.4 convolution_convert_fusion.2
  117.6 22.3 %reduce-scatter.2.cloned.1.call-done = bf16[64,1536]{1,0:T(8,128)(2,1)} async-done(((bf16[256,1536]{1,0:T(8,128)(2,1)}), bf16[64,1536]{1,0:T(8,128)(2,1)}) %reduce-scatter.2.cloned.1.call-update) | async-done | bytes 196624 | tf_op jit(solution)/shard_map/reduce_scatter | solution.py:153
  145.2 83.3 %all_to_all.29 = bf16[64,16,1536]{2,1,0:T(8,128)(2,1)S(1)} all-to-all(bf16[64,16,1536]{2,1,0:T(8,128)(2,1)S(1)} %bitcast.71), channel_id=1, replica_groups=mesh['head'=4,'blk'=64] {'blk'}, dimensions={0} | all-to-all | bytes 6291456 | tf_op jit(solution)/shard_map/all_to_all | solution.py:184
  228.5 2.6 fusion.13
  232.3 3.5 %convolution_convert_fusion = bf16[64,16,1536]{2,1,0:T(8,128)(2,1)} fusion(bf16[64,16,384]{2,1,0:T(8,128)(2,1)S(1)} %bitcast.77, bf16[1,384,1536]{2,1,0:T(8,128)(2,1)S(1)} %copy-done.48), kind=kOutput, calls=%fused_computation.16 | convolution fusion | flops 1209532416 | bytes 5111808 | tf_op jit(solution)/shard_map/dot_general | solution.py:48
  235.8 7.0 %all-to-all-start.1 = ((bf16[64,16,1536]{2,1,0:T(8,128)(2,1)}), bf16[64,16,1536]{2,1,0:T(8,128)(2,1)}, u32[]{:S(2)}, u32[]{:S(2)}) async-start(bf16[64,16,1536]{2,1,0:T(8,128)(2,1)} %convolution_convert_fusion), calls=%async_computation.2 | async-start | bytes 6291456 | tf_op jit(solution)/shard_map/all_to_all | solution.py:190
  243.2 71.2 %all-to-all-done.1 = bf16[64,16,1536]{2,1,0:T(8,128)(2,1)} async-done(((bf16[64,16,1536]{2,1,0:T(8,128)(2,1)}), bf16[64,16,1536]{2,1,0:T(8,128)(2,1)}, u32[]{:S(2)}, u32[]{:S(2)}) %all-to-all-start.1) | async-done | bytes 3145760 | tf_op jit(solution)/shard_map/all_to_all | solution.py:190
  314.5 4.2 %bitcast_reduce_fusion = bf16[32,16,1536]{2,1,0:T(8,128)(2,1)} fusion(bf16[64,16,1536]{2,1,0:T(8,128)(2,1)} %all-to-all-done.1), kind=kLoop, calls=%fused_computation.17 | loop fusion | flops 786432 | bytes 4718592 | tf_op jit(solution)/shard_map/reduce_sum | solution.py:194
  318.7 3.6 %gather_fusion = bf16[256,1536]{1,0:T(8,128)(2,1)S(1)} fusion(bf16[512,1536]{1,0:T(8,128)(2,1)} %bitcast.69, s32[1024]{0:T(1024)S(1)} %pad_clamp_fusion), kind=kCustom, calls=%fused_computation | custom fusion | bytes 1573888 | tf_op jit(solution)/shard_map/gather | solution.py:198
  323.9 2.5 multiply_reduce_fusion
  326.5 9.6 %all_to_all.30 = bf16[64,4,384]{2,0,1:T(8,128)(2,1)S(1)} all-to-all(bf16[64,4,384]{2,0,1:T(8,128)(2,1)S(1)} %bitcast.74), channel_id=1, replica_groups=mesh['head'=4,'blk'=64] {'head'}, dimensions={1} | all-to-all | bytes 393216 | tf_op jit(solution)/shard_map/all_to_all | solution.py:201
  (232 shorter events, 51.0 us)
Async XLA Ops:
  6.5 221.9 %copy-start = (bf16[1,1536,768]{2,1,0:T(8,128)(2,1)S(1)}, bf16[1,1536,768]{2,1,0:T(8,128)(2,1)}, u32[]{:S(2)}) copy-start(bf16[1,1536,768]{2,1,0:T(8,128)(2,1)} %param.21) | copy-start | bytes 7077892
  6.5 82.8 %all-gather.3.cloned.1.call-start = ((), (), s32[]{:S(2)}) async-start(), calls=%async_computation.5 | async-start | bytes 2129920 | tf_op jit(solution)/shard_map/all_gather | solution.py:140
  8.2 131.6 %reduce-scatter.2.cloned.1.call-start = ((), (), s32[]{:S(2)}) async-start(), calls=%async_computation.4 | async-start | bytes 983040 | tf_op jit(solution)/shard_map/reduce_scatter | solution.py:153
  14.8 9.9 %collective-permute-start = (bf16[256,256]{0,1:T(8,128)(2,1)}, bf16[256,256]{0,1:T(8,128)(2,1)}, u32[]{:S(2)}, u32[]{:S(2)}) collective-permute-start(bf16[256,256]{0,1:T(8,128)(2,1)} %pad_maximum_fusion), channel_id=1, source_target_pairs={{0,1},{1,2},{2,3},{3,4},{4,5},{5,6},{6,7},{7,8},{8,9},{9,10},{10,1... | collective-permute-start | bytes 393224 | tf_op jit(solution)/shard_map/ppermute | solution.py:14
  20.4 8.3 %copy-start.32 = (s32[256]{0:T(256)S(1)}, s32[256]{0:T(256)}, u32[]{:S(2)}) copy-start(s32[256]{0:T(256)} %copy-done.31) | copy-start | bytes 3076
  22.6 10.6 %copy-start.30 = (s32[256]{0:T(256)S(1)}, s32[256]{0:T(256)}, u32[]{:S(2)}) copy-start(s32[256]{0:T(256)} %copy-done.29) | copy-start | bytes 3076
  22.6 10.6 %copy-start.41 = (s32[256]{0:T(256)S(1)}, s32[256]{0:T(256)}, u32[]{:S(2)}) copy-start(s32[256]{0:T(256)} %get-tuple-element.151) | copy-start | bytes 3076
  24.7 14.9 %copy-start.28 = (s32[256]{0:T(256)S(1)}, s32[256]{0:T(256)}, u32[]{:S(2)}) copy-start(s32[256]{0:T(256)} %copy-done.27) | copy-start | bytes 3076
  24.7 14.9 %copy-start.40 = (s32[256]{0:T(256)S(1)}, s32[256]{0:T(256)}, u32[]{:S(2)}) copy-start(s32[256]{0:T(256)} %get-tuple-element.152) | copy-start | bytes 3076
  24.7 75.3 %copy-start.46 = (pred[256]{0:T(512)(128)(4,1)}, pred[256]{0:T(512)(128)(4,1)S(1)}, u32[]{:S(2)}) copy-start(pred[256]{0:T(512)(128)(4,1)S(1)} %broadcast_compare_fusion) | copy-start | bytes 772
  24.7 6.5 %collective-permute-start.1 = (bf16[256,256]{0,1:T(8,128)(2,1)}, bf16[256,256]{0,1:T(8,128)(2,1)S(1)}, u32[]{:S(2)}, u32[]{:S(2)}) collective-permute-start(bf16[256,256]{0,1:T(8,128)(2,1)} %collective-permute-done), channel_id=1, source_target_pairs={{0,1},{1,2},{2,3},{3,4},{4,5},{5,6},{6,7},{7,8},{8,9},{9,10},{10,1... | collective-permute-start | bytes 393224 | tf_op jit(solution)/shard_map/ppermute | solution.py:14
  30.8 15.2 %copy-start.26 = (s32[256]{0:T(256)S(1)}, s32[256]{0:T(256)}, u32[]{:S(2)}) copy-start(s32[256]{0:T(256)} %copy-done.25) | copy-start | bytes 3076
  30.8 15.2 %copy-start.39 = (s32[256]{0:T(256)S(1)}, s32[256]{0:T(256)}, u32[]{:S(2)}) copy-start(s32[256]{0:T(256)} %get-tuple-element.153) | copy-start | bytes 3076
  31.2 6.4 %collective-permute-start.2 = (bf16[256,256]{0,1:T(8,128)(2,1)S(1)}, bf16[256,256]{0,1:T(8,128)(2,1)S(1)}, u32[]{:S(2)}, u32[]{:S(2)}) collective-permute-start(bf16[256,256]{0,1:T(8,128)(2,1)S(1)} %collective-permute-done.1), channel_id=1, source_target_pairs={{0,1},{1,2},{2,3},{3,4},{4,5},{5,6},{6,7},{7,8},{8,9},{9,10},{10,1... | collective-permute-start | bytes 393224 | tf_op jit(solution)/shard_map/ppermute | solution.py:14
  34.4 17.8 %copy-start.24 = (s32[256]{0:T(256)S(1)}, s32[256]{0:T(256)}, u32[]{:S(2)}) copy-start(s32[256]{0:T(256)} %copy-done.23) | copy-start | bytes 3076
  34.4 17.8 %copy-start.38 = (s32[256]{0:T(256)S(1)}, s32[256]{0:T(256)}, u32[]{:S(2)}) copy-start(s32[256]{0:T(256)} %get-tuple-element.154) | copy-start | bytes 3076
  37.6 6.4 %collective-permute-start.3 = (bf16[256,256]{0,1:T(8,128)(2,1)S(1)}, bf16[256,256]{0,1:T(8,128)(2,1)S(1)}, u32[]{:S(2)}, u32[]{:S(2)}) collective-permute-start(bf16[256,256]{0,1:T(8,128)(2,1)S(1)} %collective-permute-done.2), channel_id=1, source_target_pairs={{0,1},{1,2},{2,3},{3,4},{4,5},{5,6},{6,7},{7,8},{8,9},{9,10},{10,1... | collective-permute-start | bytes 393224 | tf_op jit(solution)/shard_map/ppermute | solution.py:14
  40.8 17.7 %copy-start.22 = (s32[256]{0:T(256)S(1)}, s32[256]{0:T(256)}, u32[]{:S(2)}) copy-start(s32[256]{0:T(256)} %copy-done.21) | copy-start | bytes 3076
  40.8 17.7 %copy-start.37 = (s32[256]{0:T(256)S(1)}, s32[256]{0:T(256)}, u32[]{:S(2)}) copy-start(s32[256]{0:T(256)} %get-tuple-element.155) | copy-start | bytes 3076
  44.0 15.8 %copy-start.49 = (bf16[256,256]{0,1:T(8,128)(2,1)}, bf16[256,256]{0,1:T(8,128)(2,1)S(1)}, u32[]{:S(2)}) copy-start(bf16[256,256]{0,1:T(8,128)(2,1)S(1)} %collective-permute-done.3) | copy-start | bytes 393220
  44.0 6.3 %collective-permute-start.4 = (bf16[256,256]{0,1:T(8,128)(2,1)S(1)}, bf16[256,256]{0,1:T(8,128)(2,1)S(1)}, u32[]{:S(2)}, u32[]{:S(2)}) collective-permute-start(bf16[256,256]{0,1:T(8,128)(2,1)S(1)} %collective-permute-done.3), channel_id=1, source_target_pairs={{0,1},{1,2},{2,3},{3,4},{4,5},{5,6},{6,7},{7,8},{8,9},{9,10},{10,1... | collective-permute-start | bytes 393224 | tf_op jit(solution)/shard_map/ppermute | solution.py:14
  47.3 18.0 %copy-start.20 = (s32[256]{0:T(256)S(1)}, s32[256]{0:T(256)}, u32[]{:S(2)}) copy-start(s32[256]{0:T(256)} %copy-done.19) | copy-start | bytes 3076
  47.3 18.0 %copy-start.36 = (s32[256]{0:T(256)S(1)}, s32[256]{0:T(256)}, u32[]{:S(2)}) copy-start(s32[256]{0:T(256)} %get-tuple-element.156) | copy-start | bytes 3076
  50.3 16.2 %copy-start.51 = (bf16[256,256]{0,1:T(8,128)(2,1)}, bf16[256,256]{0,1:T(8,128)(2,1)S(1)}, u32[]{:S(2)}) copy-start(bf16[256,256]{0,1:T(8,128)(2,1)S(1)} %collective-permute-done.4) | copy-start | bytes 393220
  50.3 6.3 %collective-permute-start.5 = (bf16[256,256]{0,1:T(8,128)(2,1)S(1)}, bf16[256,256]{0,1:T(8,128)(2,1)S(1)}, u32[]{:S(2)}, u32[]{:S(2)}) collective-permute-start(bf16[256,256]{0,1:T(8,128)(2,1)S(1)} %collective-permute-done.4), channel_id=1, source_target_pairs={{0,1},{1,2},{2,3},{3,4},{4,5},{5,6},{6,7},{7,8},{8,9},{9,10},{10,1... | collective-permute-start | bytes 393224 | tf_op jit(solution)/shard_map/ppermute | solution.py:14
  53.5 17.1 %copy-start.17 = (s32[256]{0:T(256)S(1)}, s32[256]{0:T(256)}, u32[]{:S(2)}) copy-start(s32[256]{0:T(256)} %copy-done.16) | copy-start | bytes 3076
  53.5 17.1 %copy-start.34 = (s32[256]{0:T(256)S(1)}, s32[256]{0:T(256)}, u32[]{:S(2)}) copy-start(s32[256]{0:T(256)} %get-tuple-element.149) | copy-start | bytes 3076
  56.6 13.3 %copy-start.55 = (bf16[256,256]{0,1:T(8,128)(2,1)}, bf16[256,256]{0,1:T(8,128)(2,1)S(1)}, u32[]{:S(2)}) copy-start(bf16[256,256]{0,1:T(8,128)(2,1)S(1)} %collective-permute-done.5) | copy-start | bytes 393220
  56.6 6.7 %collective-permute-start.6 = (bf16[256,256]{0,1:T(8,128)(2,1)S(1)}, bf16[256,256]{0,1:T(8,128)(2,1)S(1)}, u32[]{:S(2)}, u32[]{:S(2)}) collective-permute-start(bf16[256,256]{0,1:T(8,128)(2,1)S(1)} %collective-permute-done.5), channel_id=1, source_target_pairs={{0,1},{1,2},{2,3},{3,4},{4,5},{5,6},{6,7},{7,8},{8,9},{9,10},{10,1... | collective-permute-start | bytes 393224 | tf_op jit(solution)/shard_map/ppermute | solution.py:14
  63.4 6.6 %collective-permute-start.7 = (bf16[256,256]{0,1:T(8,128)(2,1)S(1)}, bf16[256,256]{0,1:T(8,128)(2,1)S(1)}, u32[]{:S(2)}, u32[]{:S(2)}) collective-permute-start(bf16[256,256]{0,1:T(8,128)(2,1)S(1)} %collective-permute-done.6), channel_id=1, source_target_pairs={{0,1},{1,2},{2,3},{3,4},{4,5},{5,6},{6,7},{7,8},{8,9},{9,10},{10,1... | collective-permute-start | bytes 393224 | tf_op jit(solution)/shard_map/ppermute | solution.py:14
  113.8 27.3 %copy-start.33 = (f32[1536]{0:T(1024)S(1)}, f32[1536]{0:T(1024)}, u32[]{:S(2)}) copy-start(f32[1536]{0:T(1024)} %param.20) | copy-start | bytes 18436
  235.8 78.7 %all-to-all-start.1 = ((bf16[64,16,1536]{2,1,0:T(8,128)(2,1)}), bf16[64,16,1536]{2,1,0:T(8,128)(2,1)}, u32[]{:S(2)}, u32[]{:S(2)}) async-start(bf16[64,16,1536]{2,1,0:T(8,128)(2,1)} %convolution_convert_fusion), calls=%async_computation.2 | async-start | bytes 6291456 | tf_op jit(solution)/shard_map/all_to_all | solution.py:190
  (39 other events, 128.8 us)
Sparse Core Ops, SparseCore 0:
  10.1 79.1 all-gather.2
  116.4 23.4 reduce-scatter.1
where the time goes:
time: 346 us; the launch traced here: 344 us
  waiting for transfers between devices  131 us (38%)
  blocking collectives  92.9 us (27%)
  matrix products  41.4 us (12%)
  starting transfers between devices  24.3 us (7%)
  other arithmetic  20.7 us (6%)
  local copies, waits for them, and re-layouts  18.8 us (5%)
  between operations  14.6 us (4%)
    all_to_all x1, blocking collectives, shards(): lax.all_to_all(outgoing, 'blk', split_axis=0, concat_axis=0, tiled=True)  83.3 us
    all_to_all x1, waiting for transfers between devices, shards(): lax.all_to_all(partial_value.astype(jnp.bfloat16), 'blk', split_axis=0, c...  71.2 us
    dot_general x16, matrix products, matmul(): return jnp.dot(left, right, preferred_element_type=jnp.float32)  23.6 us
    reduce_scatter x1, waiting for transfers between devices, shards(): lax.psum_scatter(matmul(context, w_out).astype(jnp.bfloat16), 'head', sca...  22.3 us
    ppermute x8, waiting for transfers between devices, passed_along(): return lax.ppermute(value, axis, pairs)  19.8 us
    all_gather x1, waiting for transfers between devices, shards(): lax.all_gather(cached, 'blk', axis=0, tiled=True)  17.5 us
    ppermute x8, starting transfers between devices, passed_along(): return lax.ppermute(value, axis, pairs)  17.3 us
    dot_general x11, matrix products, attend(): lax.dot_general(queries, keys, (((1,), (1,)), ((), ())), preferred_elemen...  17.1 us
  transfers between devices with their start and end apart: 11, of which 10 were waited for; matrix products, arithmetic and copies ran while one was open for 8% of the time, Pallas kernels for 0%

commit v1 on v0

--- a/solution.py
+++ b/solution.py
@@ -1,6 +1,9 @@
+import functools
 import jax
 import jax.numpy as jnp
 from jax import lax
+from jax.experimental import pallas as pl
+from jax.experimental.pallas import tpu as pltpu
 from jax.sharding import PartitionSpec as P
 
 KVH = 2
@@ -79,6 +82,419 @@
     if width == count:
         return one_part(0, state)
     return lax.fori_loop(0, count // width, one_part, state)
+
+
+MESH = pl.DeviceIdType.MESH
+CORES = 2
+ROWS_BLOCK = 64
+PIECE = 16
+ORDER = (0, 7, 1, 6, 2, 5, 3, 4)
+PLACE = {rel: at for at, rel in enumerate(ORDER)}
+
+
+def moe_kernel(
+    sizes,
+    mid_ref,
+    gain_ref,
+    routes_ref,
+    weights_ref,
+    gateup_ref,
+    down_ref,
+    out_ref,
+    tokens,
+    table,
+    tables,
+    packed,
+    rows,
+    outs,
+    backs,
+    gate_up,
+    down,
+    partial,
+    sums_r,
+    sums_l,
+    got_r,
+    got_l,
+    final,
+    landed,
+    local_sem,
+    wsend,
+    wrecv,
+    tsend,
+    trecv,
+    zsend,
+    zrecv,
+    ysend,
+    yrecv,
+    bsend,
+    brecv,
+    ssend,
+    srecv,
+    xsend,
+    xrecv,
+):
+    xs, ys, zs = sizes
+    head = lax.axis_index("head")
+    blk = lax.axis_index("blk")
+    core = blk % CORES
+    z = (blk // CORES) % zs
+    y = blk // (CORES * zs)
+    width = mid_ref.shape[1]
+    half_units = down.shape[1]
+    chunk = ROWS_BLOCK // 2
+
+    def at(dx=0, dy=0, dz=0, other=False):
+        hx = (head + dx) % xs
+        yy = (y + dy) % ys
+        zz = (z + dz) % zs
+        cc = 1 - core if other else core
+        return (hx, (yy * zs + zz) * CORES + cc)
+
+    peers = (
+        [at(other=True)]
+        + [at(dz=d) for d in range(1, zs)]
+        + [at(dy=d) for d in range(1, ys)]
+        + [at(dx=d) for d in range(1, xs)]
+    )
+    barrier = pltpu.get_barrier_semaphore()
+    for peer in peers:
+        pl.semaphore_signal(barrier, inc=1, device_id=peer, device_id_type=MESH)
+
+    own_copies = [
+        pltpu.make_async_copy(gateup_ref.at[0], gate_up.at[0], local_sem.at[0]),
+        pltpu.make_async_copy(down_ref.at[0], down.at[0], local_sem.at[1]),
+    ]
+    for copy in own_copies:
+        copy.start()
+    wide = mid_ref[...].astype(jnp.float32)
+    scale = lax.rsqrt(jnp.mean(wide * wide, axis=-1, keepdims=True) + 1e-05)
+    tokens[0] = (wide * scale * gain_ref[...]).astype(jnp.bfloat16)
+    lanes = routes_ref.shape[1]
+    row = lax.broadcasted_iota(jnp.int32, (zs * 2 * ys, lanes), 0)
+    part = row % (2 * ys)
+    expert = ((y + part % ys) % ys) * zs + row // (2 * ys)
+    hit = jnp.zeros((zs * 2 * ys, lanes), jnp.float32)
+    weight = jnp.zeros((zs * 2 * ys, lanes), jnp.float32)
+    for k in range(routes_ref.shape[0]):
+        same = routes_ref[k : k + 1, :] == expert
+        hit = hit + jnp.where(same, 1.0, 0.0)
+        weight = weight + jnp.where(same, weights_ref[k : k + 1, :], 0.0)
+    before = jnp.where(
+        lax.broadcasted_iota(jnp.int32, (lanes, lanes), 0)
+        < lax.broadcasted_iota(jnp.int32, (lanes, lanes), 1),
+        1.0,
+        0.0,
+    )
+    rank = jnp.dot(
+        hit.astype(jnp.bfloat16),
+        before.astype(jnp.bfloat16),
+        preferred_element_type=jnp.float32,
+    )
+    code = jnp.where(hit > 0.5, rank, -1.0)
+    table[...] = jnp.where(part < ys, code, weight).reshape(zs, 2 * ys, lanes)
+    pl.semaphore_wait(barrier, len(peers))
+
+    table_copies = {}
+    for d in range(1, zs):
+        table_copies[d] = pltpu.make_async_remote_copy(
+            src_ref=table.at[(z + d) % zs],
+            dst_ref=tables.at[PLACE[zs - d]],
+            send_sem=tsend.at[d],
+            recv_sem=trecv.at[zs - d],
+            device_id=at(dz=d),
+            device_id_type=MESH,
+        )
+        table_copies[d].start()
+
+    def token_copy(direction, step, piece):
+        held = (-step * direction) % zs
+        there = (held - direction) % zs
+        number = step * 2 + piece
+        side = 0 if direction == 1 else 1
+        return pltpu.make_async_remote_copy(
+            src_ref=tokens.at[PLACE[held], pl.ds(piece * chunk, chunk)],
+            dst_ref=tokens.at[PLACE[there], pl.ds(piece * chunk, chunk)],
+            send_sem=zsend.at[side, number],
+            recv_sem=zrecv.at[side, number],
+            device_id=at(dz=direction),
+            device_id_type=MESH,
+        )
+
+    reach = zs // 2
+    flow = {}
+    for direction in (1, -1):
+        for step in range(reach):
+            for piece in range(2):
+                if step < reach - 1 or piece == (0 if direction == 1 else 1):
+                    flow[direction, step, piece] = token_copy(direction, step, piece)
+
+    for piece in range(2):
+        flow[1, 0, piece].start()
+        flow[-1, 0, piece].start()
+
+    weight_copies = [
+        pltpu.make_async_remote_copy(
+            src_ref=gateup_ref.at[0],
+            dst_ref=gate_up.at[1],
+            send_sem=wsend.at[0],
+            recv_sem=wrecv.at[0],
+            device_id=at(other=True),
+            device_id_type=MESH,
+        ),
+        pltpu.make_async_remote_copy(
+            src_ref=down_ref.at[0],
+            dst_ref=down.at[1],
+            send_sem=wsend.at[1],
+            recv_sem=wrecv.at[1],
+            device_id=at(other=True),
+            device_id_type=MESH,
+        ),
+    ]
+    for copy in weight_copies:
+        copy.start()
+
+    slot = lax.broadcasted_iota(jnp.int32, (ys * PIECE, lanes), 0) % PIECE
+    slot = slot.astype(jnp.float32)
+
+    def spread(place, first):
+        return jnp.concatenate(
+            [
+                jnp.broadcast_to(tables[place, first + dy : first + dy + 1, :], (PIECE, lanes))
+                for dy in range(ys)
+            ],
+            axis=0,
+        )
+
+    def piece_copy(place, dy):
+        return pltpu.make_async_remote_copy(
+            src_ref=packed.at[place, dy],
+            dst_ref=rows.at[place, ys - dy],
+            send_sem=ysend.at[place, dy],
+            recv_sem=yrecv.at[place, ys - dy],
+            device_id=at(dy=dy),
+            device_id_type=MESH,
+        )
+
+    def back_copy(place, dy):
+        return pltpu.make_async_remote_copy(
+            src_ref=outs.at[place, dy],
+            dst_ref=backs.at[place, ys - dy],
+            send_sem=bsend.at[place, dy],
+            recv_sem=brecv.at[place, ys - dy],
+            device_id=at(dy=dy),
+            device_id_type=MESH,
+        )
+
+    def arrival(make, sems, place, dy):
+        copy = make(place, ys - dy)
+        copy.wait_recv()
+
+    def pack(place):
+        if place > 0:
+            table_copies[(zs - ORDER[place])].wait_recv()
+        chosen = jnp.where(spread(place, 0) == slot, 1.0, 0.0).astype(jnp.bfloat16)
+        value = jnp.dot(
+            chosen[:, :ROWS_BLOCK], tokens[place], preferred_element_type=jnp.float32
+        ).astype(jnp.bfloat16)
+        value = value.reshape(ys, PIECE, width)
+        packed[place, 1:] = value[1:]
+        rows[place, 0] = value[0]
+        for dy in (2, 1, 3):
+            piece_copy(place, dy).start()
+
+    def experts(first, count):
+        for place in range(first, first + count):
+            for dy in range(1, ys):
+                arrival(piece_copy, yrecv, place, dy)
+        taken = rows[first : first + count].reshape(count * ys * PIECE, width)
+        total = None
+        for side in range(2):
+            both = jnp.dot(taken, gate_up[side], preferred_element_type=jnp.float32)
+            hidden = jax.nn.relu(both[:, :half_units]) * both[:, half_units:]
+            term = jnp.dot(
+                hidden.astype(jnp.bfloat16), down[side], preferred_element_type=jnp.float32
+            )
+            total = term if total is None else total + term
+        value = total.astype(jnp.bfloat16).reshape(count, ys, PIECE, width)
+        outs[first : first + count, 1:] = value[:, 1:]
+        backs[first : first + count, 0] = value[:, 0]
+        for place in range(first, first + count):
+            for dy in (2, 1, 3):
+                back_copy(place, dy).start()
+
+    def combine(place):
+        for dy in range(1, ys):
+            arrival(back_copy, brecv, place, dy)
+        mixing = jnp.where(spread(place, 0) == slot, spread(place, ys), 0.0)
+        mixing = mixing.astype(jnp.bfloat16)[:, :ROWS_BLOCK]
+        partial[place] = lax.dot_general(
+            mixing,
+            backs[place].reshape(ys * PIECE, width),
+            (((0,), (0,)), ((), ())),
+            preferred_element_type=jnp.float32,
+        )
+
+    tables[0] = table[z]
+    pack(0)
+    for step in range(1, reach + 1):
+        for piece in range(2):
+            for direction in (1, -1):
+                if (direction, step - 1, piece) in flow:
+                    flow[direction, step - 1, piece].wait_recv()
+                if (direction, step, piece) in flow:
+                    flow[direction, step, piece].start()
+        if step < reach:
+            pack(PLACE[zs - step])
+            pack(PLACE[step])
+        else:
+            pack(PLACE[reach])
+        if step == 1:
+            for copy in own_copies:
+                copy.wait()
+            for copy in weight_copies:
+                copy.wait_recv()
+            experts(0, 1)
+        else:
+            experts(PLACE[zs - step + 1], 2)
+    experts(PLACE[reach], 1)
+    for place in range(5):
+        combine(place)
+
+    def sum_copy(direction, held, piece):
+        side = 0 if direction == 1 else 1
+        number = (held if direction == 1 else zs - held) * 2 + piece
+        source, target = (sums_r, got_r) if direction == 1 else (sums_l, got_l)
+        return pltpu.make_async_remote_copy(
+            src_ref=source.at[number],
+            dst_ref=target.at[number],
+            send_sem=ssend.at[side, number],
+            recv_sem=srecv.at[side, number],
+            device_id=at(dz=direction),
+            device_id_type=MESH,
+        )
+
+    returned = {}
+
+    def pass_on(direction, distance, piece):
+        held = distance if direction == 1 else zs - distance
+        number = distance * 2 + piece
+        value = partial[PLACE[held], pl.ds(piece * chunk, chunk)]
+        source, target = (sums_r, got_r) if direction == 1 else (sums_l, got_l)
+        if (direction, distance + 1, piece) in returned:
+            returned[direction, distance + 1, piece].wait_recv()
+            value = value + target[number + 2].astype(jnp.float32)
+        source[number] = value.astype(jnp.bfloat16)
+        copy = sum_copy(direction, held, piece)
+        returned[direction, distance, piece] = copy
+        copy.start()
+
+    combine(PLACE[reach - 1])
+    pass_on(1, reach - 1, 1)
+    combine(PLACE[zs - reach + 1])
+    pass_on(-1, reach - 1, 0)
+    combine(PLACE[reach])
+    pass_on(1, reach, 0)
+    pass_on(-1, reach, 1)
+    for distance in range(reach - 1, 0, -1):
+        if distance < reach - 1:
+            pass_on(1, distance, 1)
+            pass_on(-1, distance, 0)
+        pass_on(1, distance, 0)
+        pass_on(-1, distance, 1)
+    for piece in (1, 0):
+        spot = pl.ds(piece * chunk, chunk)
+        returned[1, 1, piece].wait_recv()
+        returned[-1, 1, piece].wait_recv()
+        value = (
+            mid_ref[spot].astype(jnp.float32)
+            + partial[0, spot]
+            + got_r[2 + piece].astype(jnp.float32)
+            + got_l[2 + piece].astype(jnp.float32)
+        ).astype(jnp.bfloat16)
+        share = width // xs
+        for part_x in range(xs):
+            final[part_x, spot] = value[:, part_x * share : (part_x + 1) * share]
+
+    last = []
+    for dx in range(1, xs):
+        copy = pltpu.make_async_remote_copy(
+            src_ref=final.at[(head + dx) % xs],
+            dst_ref=landed.at[head],
+            send_sem=xsend.at[dx],
+            recv_sem=xrecv.at[xs - dx],
+            device_id=at(dx=dx),
+            device_id_type=MESH,
+        )
+        copy.start()
+        last.append(copy)
+    out_ref[head] = final[head]
+    for dx in range(1, xs):
+        last[xs - dx - 1].wait_recv()
+        out_ref[(head + dx) % xs] = landed[(head + dx) % xs]
+
+    for copy in weight_copies + list(table_copies.values()) + list(flow.values()):
+        copy.wait_send()
+    for place in range(zs):
+        for dy in range(1, ys):
+            piece_copy(place, dy).wait_send()
+            back_copy(place, dy).wait_send()
+    for copy in list(returned.values()) + last:
+        copy.wait_send()
+
+
+def moe(sizes, middle, gain, routes, weights, w_gateup, w_down):
+    xs, ys, zs = sizes
+    count, width = middle.shape
+    lanes = 128
+    routes_t = jnp.pad(routes, ((0, lanes - count), (0, 0)), constant_values=-1).T
+    weights_t = jnp.pad(weights, ((0, lanes - count), (0, 0))).T
+    bf16, f32 = jnp.bfloat16, jnp.float32
+    dma = pltpu.SemaphoreType.DMA
+    vmem = pl.BlockSpec(memory_space=pltpu.VMEM)
+    hbm = pl.BlockSpec(memory_space=pl.ANY)
+    out = pl.pallas_call(
+        functools.partial(moe_kernel, sizes),
+        out_shape=jax.ShapeDtypeStruct((xs, count, width // xs), bf16),
+        in_specs=[vmem, vmem, vmem, vmem, hbm, hbm],
+        out_specs=vmem,
+        scratch_shapes=[
+            pltpu.VMEM((zs, count, width), bf16),
+            pltpu.VMEM((zs, 2 * ys, lanes), f32),
+            pltpu.VMEM((zs, 2 * ys, lanes), f32),
+            pltpu.VMEM((zs, ys, PIECE, width), bf16),
+            pltpu.VMEM((zs, ys, PIECE, width), bf16),
+            pltpu.VMEM((zs, ys, PIECE, width), bf16),
+            pltpu.VMEM((zs, ys, PIECE, width), bf16),
+            pltpu.VMEM((2,) + w_gateup.shape[1:], bf16),
+            pltpu.VMEM((2,) + w_down.shape[1:], bf16),
+            pltpu.VMEM((zs, count, width), f32),
+            pltpu.VMEM((zs + 2, count // 2, width), bf16),
+            pltpu.VMEM((zs + 2, count // 2, width), bf16),
+            pltpu.VMEM((zs + 2, count // 2, width), bf16),
+            pltpu.VMEM((zs + 2, count // 2, width), bf16),
+            pltpu.VMEM((xs, count, width // xs), bf16),
+            pltpu.VMEM((xs, count, width // xs), bf16),
+            dma((2,)),
+            dma((2,)),
+            dma((2,)),
+            dma((zs,)),
+            dma((zs,)),
+            dma((2, zs)),
+            dma((2, zs)),
+            dma((zs, ys)),
+            dma((zs, ys)),
+            dma((zs, ys)),
+            dma((zs, ys)),
+            dma((2, zs + 2)),
+            dma((2, zs + 2)),
+            dma((xs,)),
+            dma((xs,)),
+        ],
+        compiler_params=pltpu.CompilerParams(
+            collective_id=1, has_side_effects=True, vmem_limit_bytes=60 * 2**20
+        ),
+    )(middle, gain.reshape(1, width), routes_t, weights_t, w_gateup, w_down)
+    return out.reshape(xs * count, width // xs)
 
 
 def shards(
@@ -155,50 +571,11 @@
     ).astype(jnp.float32)
     resid = lax.dynamic_slice_in_dim(hidden_in, head_index * quarter, quarter, 0)
     middle = (resid.astype(jnp.float32) + attn_share).astype(jnp.bfloat16)
-    moe_in = rms_norm(middle, moe_gain).astype(jnp.bfloat16)
     my_routes = lax.dynamic_slice_in_dim(routes, head_index * quarter, quarter, 0)
     my_weights = lax.dynamic_slice_in_dim(route_weights, head_index * quarter, quarter, 0)
-    expert_count = block_count // 2
-    capacity = max(2, min(2 * quarter * TOPK // expert_count, quarter))
-    width_d = moe_in.shape[1]
-    flat_ids = my_routes.reshape(-1)
-    onehot = (flat_ids[:, None] == jnp.arange(expert_count, dtype=jnp.int32)[None, :]).astype(
-        jnp.int32
-    )
-    slots = jnp.sum((jnp.cumsum(onehot, axis=0) - 1) * onehot, axis=1)
-    target = flat_ids * capacity + slots
-    table = (
-        target[:, None] == jnp.arange(expert_count * capacity, dtype=jnp.int32)[None, :]
-    ).astype(jnp.bfloat16)
-    repeated = jnp.repeat(moe_in, TOPK, axis=0)
-    packed = lax.dot_general(
-        table, repeated, (((0,), (0,)), ((), ())), preferred_element_type=jnp.float32
-    ).astype(jnp.bfloat16)
-    gate_up = w_gateup[0]
-    down = w_down[0]
-    half_units = down.shape[0]
-    doubled = jnp.broadcast_to(
-        packed.reshape(expert_count, 1, capacity, width_d), (expert_count, 2, capacity, width_d)
-    )
-    outgoing = doubled.reshape(2 * expert_count, capacity, width_d)
-    received = lax.all_to_all(outgoing, "blk", split_axis=0, concat_axis=0, tiled=True)
-    senders, count, depth = received.shape
-    rows = received.reshape(senders * count, depth)
-    both = matmul(rows, gate_up)
-    hidden = (jax.nn.relu(both[:, :half_units]) * both[:, half_units:]).astype(jnp.bfloat16)
-    partial_value = matmul(hidden, down).reshape(senders, count, depth)
-    back = lax.all_to_all(
-        partial_value.astype(jnp.bfloat16), "blk", split_axis=0, concat_axis=0, tiled=True
-    ).astype(partial_value.dtype)
-    outputs = (
-        jnp.sum(back.reshape(expert_count, 2, capacity, width_d), axis=1)
-        .astype(jnp.bfloat16)
-        .reshape(expert_count * capacity, width_d)
-    )
-    picked = outputs[target].astype(jnp.float32).reshape(quarter, TOPK, width_d)
-    mixed = jnp.sum(picked * my_weights[:, :, None], axis=1)
-    final = (middle.astype(jnp.float32) + mixed).astype(jnp.bfloat16)
-    return lax.all_to_all(final, "head", split_axis=1, concat_axis=0, tiled=True)
+    chips_z = 8
+    sizes = (head_count, block_count // (CORES * chips_z), chips_z)
+    return moe(sizes, middle, moe_gain, my_routes, my_weights, w_gateup, w_down)
 
 
 def solution(mesh):

time: 346 us -> 221 us (0.64)
  blocking collectives: 92.9 us -> 0 us
  Pallas kernels: 0 us -> 72.6 us
  waiting for transfers between devices: 131 us -> 64.9 us
  matrix products: 41.4 us -> 31.1 us
  local copies, waits for them, and re-layouts: 18.8 us -> 8.6 us
  other arithmetic: 20.7 us -> 11.2 us
  starting transfers between devices: 24.3 us -> 17.5 us
    all_to_all x2 -> x0, blocking collectives: 92.9 us -> none  [the longest x1 83.3 us: shards(): lax.all_to_all(outgoing, 'blk', split_axis=0, concat_axis=0, tiled=True)]
    pallas_call x0 -> x1, Pallas kernels: none -> 72.6 us  [moe(): pl.pallas_call(functools.partial(moe_kernel, sizes), out_shape=jax.ShapeD...]
    all_to_all x1 -> x0, waiting for transfers between devices: 71.2 us -> none  [shards(): lax.all_to_all(partial_value.astype(jnp.bfloat16), 'blk', split_axis=0, c...]
    dot_general x16 -> x14, matrix products: 23.6 us -> 15.7 us  [matmul(): return jnp.dot(left, right, preferred_element_type=jnp.float32)]
    all_to_all x1 -> x0, starting transfers between devices: 7 us -> none  [shards(): lax.all_to_all(partial_value.astype(jnp.bfloat16), 'blk', split_axis=0, c...]
    reduce_sum x3 -> x0, other arithmetic: 6.8 us -> none  [the longest x1 4.18 us: shards(): jnp.sum(back.reshape(expert_count, 2, capacity, width_d), axis=1)]
    all_gather x1, waiting for transfers between devices: 17.5 us -> 23.2 us  [shards(): lax.all_gather(cached, 'blk', axis=0, tiled=True)]
    gather x1 -> x0, local copies, waits for them, and re-layouts: 3.6 us -> none  [shards(): picked = outputs[target].astype(jnp.float32).reshape(quarter, TOPK, width_d)]
  transfers between devices with their start and end apart: 11 -> 10, of which waited for: 10 -> 9; matrix products, arithmetic and copies ran while one was open for 8% -> 10% of each run, Pallas kernels for 0% -> 0%
where the time goes in v1:
time: 221 us; the launch traced here: 220 us
  Pallas kernels  72.6 us (33%)
  waiting for transfers between devices  64.9 us (29%)
  matrix products  31.1 us (14%)
  starting transfers between devices  17.5 us (8%)
  between operations  14.2 us (6%)
  other arithmetic  11.2 us (5%)
  local copies, waits for them, and re-layouts  8.6 us (4%)
    pallas_call x1, Pallas kernels, moe(): pl.pallas_call(functools.partial(moe_kernel, sizes), out_shape=jax.ShapeD...  72.6 us
    all_gather x1, waiting for transfers between devices, shards(): lax.all_gather(cached, 'blk', axis=0, tiled=True)  23.2 us
    reduce_scatter x1, waiting for transfers between devices, shards(): lax.psum_scatter(matmul(context, w_out).astype(jnp.bfloat16), 'head', sca...  21.7 us
    ppermute x8, waiting for transfers between devices, passed_along(): return lax.ppermute(value, axis, pairs)  20 us
    ppermute x8, starting transfers between devices, passed_along(): return lax.ppermute(value, axis, pairs)  17.5 us
    dot_general x14, matrix products, matmul(): return jnp.dot(left, right, preferred_element_type=jnp.float32)  15.7 us
    dot_general x11, matrix products, attend(): lax.dot_general(queries, keys, (((1,), (1,)), ((), ())), preferred_elemen...  15.4 us
    reduce_sum x5, other arithmetic, attend(): total = total * rescale + jnp.sum(weights, axis=1)  6.61 us
  transfers between devices with their start and end apart: 10, of which 9 were waited for; matrix products, arithmetic and copies ran while one was open for 10% of the time, Pallas kernels for 0%

profile of v1, /device:TPU:32, one launch (start us, length us, event | category | flops | bytes accessed | tf_op | source)
XLA Modules:
  0.0 220.1 jit_solution(11972417241030772460)
XLA Ops:
  8.3 1.4 fusion.13
  9.7 1.8 fusion.26
  12.5 1.9 collective-permute-start
  15.3 1.9 fusion.76
  18.9 3.9 %collective-permute-start.1 = (bf16[256,256]{0,1:T(8,128)(2,1)}, bf16[256,256]{0,1:T(8,128)(2,1)S(1)}, u32[]{:S(2)}, u32[]{:S(2)}) collective-permute-start(bf16[256,256]{0,1:T(8,128)(2,1)} %collective-permute-done), channel_id=1, source_target_pairs={{0,1},{1,2},{2,3},{3,4},{4,5},{5,6},{6,7},{7,8},{8,9},{9,10},{10,1... | collective-permute-start | bytes 393224 | tf_op jit(solution)/shard_map/ppermute | solution.py:17
  22.8 2.1 fusion.122
  25.4 1.9 collective-permute-start.2
  28.6 3.1 %collective-permute-done.2 = bf16[256,256]{0,1:T(8,128)(2,1)S(1)} collective-permute-done((bf16[256,256]{0,1:T(8,128)(2,1)S(1)}, bf16[256,256]{0,1:T(8,128)(2,1)S(1)}, u32[]{:S(2)}, u32[]{:S(2)}) %collective-permute-start.2) | collective-permute-done | bytes 131104 | tf_op jit(solution)/shard_map/ppermute | solution.py:17
  31.7 1.9 collective-permute-start.3
  34.9 3.3 %collective-permute-done.3 = bf16[256,256]{0,1:T(8,128)(2,1)S(1)} collective-permute-done((bf16[256,256]{0,1:T(8,128)(2,1)S(1)}, bf16[256,256]{0,1:T(8,128)(2,1)S(1)}, u32[]{:S(2)}, u32[]{:S(2)}) %collective-permute-start.3) | collective-permute-done | bytes 131104 | tf_op jit(solution)/shard_map/ppermute | solution.py:17
  38.2 1.9 collective-permute-start.4
  41.4 3.2 %collective-permute-done.4 = bf16[256,256]{0,1:T(8,128)(2,1)S(1)} collective-permute-done((bf16[256,256]{0,1:T(8,128)(2,1)S(1)}, bf16[256,256]{0,1:T(8,128)(2,1)S(1)}, u32[]{:S(2)}, u32[]{:S(2)}) %collective-permute-start.4) | collective-permute-done | bytes 131104 | tf_op jit(solution)/shard_map/ppermute | solution.py:17
  44.6 1.9 collective-permute-start.5
  47.8 3.1 %collective-permute-done.5 = bf16[256,256]{0,1:T(8,128)(2,1)S(1)} collective-permute-done((bf16[256,256]{0,1:T(8,128)(2,1)S(1)}, bf16[256,256]{0,1:T(8,128)(2,1)S(1)}, u32[]{:S(2)}, u32[]{:S(2)}) %collective-permute-start.5) | collective-permute-done | bytes 131104 | tf_op jit(solution)/shard_map/ppermute | solution.py:17
  50.9 1.9 collective-permute-start.6
  54.1 3.1 %collective-permute-done.6 = bf16[256,256]{0,1:T(8,128)(2,1)S(1)} collective-permute-done((bf16[256,256]{0,1:T(8,128)(2,1)S(1)}, bf16[256,256]{0,1:T(8,128)(2,1)S(1)}, u32[]{:S(2)}, u32[]{:S(2)}) %collective-permute-start.6) | collective-permute-done | bytes 131104 | tf_op jit(solution)/shard_map/ppermute | solution.py:17
  57.2 2.1 collective-permute-start.7
  60.6 3.6 %collective-permute-done.7 = bf16[256,256]{0,1:T(8,128)(2,1)S(1)} collective-permute-done((bf16[256,256]{0,1:T(8,128)(2,1)S(1)}, bf16[256,256]{0,1:T(8,128)(2,1)S(1)}, u32[]{:S(2)}, u32[]{:S(2)}) %collective-permute-start.7) | collective-permute-done | bytes 131104 | tf_op jit(solution)/shard_map/ppermute | solution.py:17
  66.1 23.2 %all-gather.3.cloned.1.call-done = bf16[4096,1,256]{2,0,1:T(8,128)(2,1)} async-done(((bf16[64,1,256]{2,0,1:T(8,128)(2,1)}), bf16[4096,1,256]{2,0,1:T(8,128)(2,1)}) %all-gather.3.cloned.1.call-update) | async-done | bytes 2097168 | tf_op jit(solution)/shard_map/all_gather | solution.py:556
  89.3 10.6 %while.18 = (s32[]{:T(128)}, f32[768]{0:T(1024)S(1)}, f32[768]{0:T(1024)S(1)}, f32[768,128]{1,0:T(8,128)S(1)}, bf16[4096,256]{1,0:T(8,128)(2,1)}, /*index=5*/bf1...) while((s32[]{:T(128)}, f32[768]{0:T(1024)S(1)}, ...), condition=%wide.region_7.8_spmd.clone, body=%wide.region_4.7_spmd.clone.sunk | while | flops 813469440 | bytes 20955336 | solution.py:84
  89.3 2.0 fusion.148
  92.2 2.3 %fusion.151 = f32[768,128]{1,0:T(8,128)S(1)} fusion(f32[2048,768]{1,0:T(8,128)S(1)} %get-tuple-element.269, f32[768]{0:T(1024)S(1)} %select_maximum_fusion.2, bf16[4096,256]{1,0:T(8,128)(2,1)} %get-tuple-element.298, s32[]{:T(128)S(6)} %select_n.170, s32[]{:T(128)S(6)} %add.490, f32[768,128]{1,0:T(8,128)S(1)} %get-tuple-element.286, ...), kind=kOutput, calls=%fused_computation.5.clone.1 | convolution fusion | flops 406093824 | bytes 7608329 | tf_op jit(solution)/shard_map/while/body/eval_jaxpr/dot_general | solution.py:51
  94.6 2.0 fusion.148
  97.5 2.3 %fusion.151 = f32[768,128]{1,0:T(8,128)S(1)} fusion(f32[2048,768]{1,0:T(8,128)S(1)} %get-tuple-element.269, f32[768]{0:T(1024)S(1)} %select_maximum_fusion.2, bf16[4096,256]{1,0:T(8,128)(2,1)} %get-tuple-element.298, s32[]{:T(128)S(6)} %select_n.170, s32[]{:T(128)S(6)} %add.490, f32[768,128]{1,0:T(8,128)S(1)} %get-tuple-element.286, ...), kind=kOutput, calls=%fused_computation.5.clone.1 | convolution fusion | flops 406093824 | bytes 7608329 | tf_op jit(solution)/shard_map/while/body/eval_jaxpr/dot_general | solution.py:51
  99.9 2.4 %fusion.29 = (f32[768]{0:T(1024)S(1)}, f32[768]{0:T(1024)S(1)}, f32[768]{0:T(1024)S(1)}) fusion(f32[768,256]{0,1:T(8,128)S(1)} %get-tuple-element.216, f32[768]{0:T(1024)S(1)} %get-tuple-element.190, pred[256]{0:T(512)(128)(4,1)S(1)} %fusion.103, s32[768]{0:T(1024)S(1)} %le.41, s32[256]{0:T(256)S(1)} %iota_add_fusion.8, s32[256]{0:T(256)S(1)} %get-tuple-element.157, ...), kind=kLoop, calls=%fused_computation.70 | loop fusion | flops 4126464 | bytes 2390784 | tf_op jit(solution)/shard_map/reduce_sum | solution.py:68
  103.9 1.3 fusion.33
  105.9 1.4 fusion.17
  112.2 1.4 convolution_convert_fusion
  115.6 21.7 %reduce-scatter.2.cloned.1.call-done = bf16[64,1536]{1,0:T(8,128)(2,1)} async-done(((bf16[256,1536]{1,0:T(8,128)(2,1)}), bf16[64,1536]{1,0:T(8,128)(2,1)}) %reduce-scatter.2.cloned.1.call-update) | async-done | bytes 196624 | tf_op jit(solution)/shard_map/reduce_scatter | solution.py:569
  137.3 1.7 add_convert_fusion.mid_ref
  139.1 72.6 %shard_map.118 = bf16[4,64,384]{2,1,0:T(8,128)(2,1)} custom-call(bf16[64,1536]{1,0:T(8,128)(2,1)} %add_convert_fusion.mid_ref, f32[1,1536]{1,0:T(1,128)} %reshape.298.gain_ref, s32[4,128]{1,0:T(4,128)} %pad_bitcast_fusion.1.routes_ref, f32[4,128]{1,0:T(4,128)} %pad_bitcast_fusion.weights_ref, bf16[1,1536,768]{2,1,0:T(8,128)(2,1)} %gateup_ref.1, ...), custom_call_target="tpu_custom_call" | custom-call | tf_op jit(solution)/shard_map/pallas_call | solution.py:455
  211.7 1.6 copy.40
  (142 shorter events, 25.7 us)
Async XLA Ops:
  6.5 3.1 %copy-start = (bf16[2,1536,256]{2,1,0:T(8,128)(2,1)S(1)}, bf16[2,1536,256]{2,1,0:T(8,128)(2,1)}, u32[]{:S(2)}) copy-start(bf16[2,1536,256]{2,1,0:T(8,128)(2,1)} %param.17) | copy-start | bytes 4718596
  6.5 82.7 %all-gather.3.cloned.1.call-start = ((), (), s32[]{:S(2)}) async-start(), calls=%async_computation.2 | async-start | bytes 2129920 | tf_op jit(solution)/shard_map/all_gather | solution.py:556
  8.2 129.1 %reduce-scatter.2.cloned.1.call-start = ((), (), s32[]{:S(2)}) async-start(), calls=%async_computation.1 | async-start | bytes 983040 | tf_op jit(solution)/shard_map/reduce_scatter | solution.py:569
  8.3 3.3 %copy-start.14 = (s32[32]{0:T(128)S(1)}, s32[32]{0:T(128)}, u32[]{:S(2)}) copy-start(s32[32]{0:T(128)} %param.25) | copy-start | bytes 388
  9.7 5.7 %copy-start.1 = (bf16[256,1536]{1,0:T(8,128)(2,1)S(1)}, bf16[256,1536]{1,0:T(8,128)(2,1)}, u32[]{:S(2)}) copy-start(bf16[256,1536]{1,0:T(8,128)(2,1)} %param.14) | copy-start | bytes 2359300
  9.7 5.6 %copy-start.29 = (f32[1536]{0:T(1024)S(1)}, f32[1536]{0:T(1024)}, u32[]{:S(2)}) copy-start(f32[1536]{0:T(1024)} %param.15) | copy-start | bytes 18436
  12.5 6.4 %collective-permute-start = (bf16[256,256]{0,1:T(8,128)(2,1)S(1)}, bf16[256,256]{0,1:T(8,128)(2,1)}, u32[]{:S(2)}, u32[]{:S(2)}) collective-permute-start(bf16[256,256]{0,1:T(8,128)(2,1)S(1)} %pad_maximum_fusion), channel_id=1, source_target_pairs={{0,1},{1,2},{2,3},{3,4},{4,5},{5,6},{6,7},{7,8},{8,9},{9,10},{10,1... | collective-permute-start | bytes 393224 | tf_op jit(solution)/shard_map/ppermute | solution.py:17
  18.9 6.5 %collective-permute-start.1 = (bf16[256,256]{0,1:T(8,128)(2,1)}, bf16[256,256]{0,1:T(8,128)(2,1)S(1)}, u32[]{:S(2)}, u32[]{:S(2)}) collective-permute-start(bf16[256,256]{0,1:T(8,128)(2,1)} %collective-permute-done), channel_id=1, source_target_pairs={{0,1},{1,2},{2,3},{3,4},{4,5},{5,6},{6,7},{7,8},{8,9},{9,10},{10,1... | collective-permute-start | bytes 393224 | tf_op jit(solution)/shard_map/ppermute | solution.py:17
  25.4 16.0 %copy-start.15 = (bf16[256,256]{0,1:T(8,128)(2,1)}, bf16[256,256]{0,1:T(8,128)(2,1)S(1)}, u32[]{:S(2)}) copy-start(bf16[256,256]{0,1:T(8,128)(2,1)S(1)} %collective-permute-done.1) | copy-start | bytes 393220
  25.4 6.3 %collective-permute-start.2 = (bf16[256,256]{0,1:T(8,128)(2,1)S(1)}, bf16[256,256]{0,1:T(8,128)(2,1)S(1)}, u32[]{:S(2)}, u32[]{:S(2)}) collective-permute-start(bf16[256,256]{0,1:T(8,128)(2,1)S(1)} %collective-permute-done.1), channel_id=1, source_target_pairs={{0,1},{1,2},{2,3},{3,4},{4,5},{5,6},{6,7},{7,8},{8,9},{9,10},{10,1... | collective-permute-start | bytes 393224 | tf_op jit(solution)/shard_map/ppermute | solution.py:17
  31.7 16.1 %copy-start.17 = (bf16[256,256]{0,1:T(8,128)(2,1)}, bf16[256,256]{0,1:T(8,128)(2,1)S(1)}, u32[]{:S(2)}) copy-start(bf16[256,256]{0,1:T(8,128)(2,1)S(1)} %collective-permute-done.2) | copy-start | bytes 393220
  31.7 6.5 %collective-permute-start.3 = (bf16[256,256]{0,1:T(8,128)(2,1)S(1)}, bf16[256,256]{0,1:T(8,128)(2,1)S(1)}, u32[]{:S(2)}, u32[]{:S(2)}) collective-permute-start(bf16[256,256]{0,1:T(8,128)(2,1)S(1)} %collective-permute-done.2), channel_id=1, source_target_pairs={{0,1},{1,2},{2,3},{3,4},{4,5},{5,6},{6,7},{7,8},{8,9},{9,10},{10,1... | collective-permute-start | bytes 393224 | tf_op jit(solution)/shard_map/ppermute | solution.py:17
  38.2 15.9 %copy-start.19 = (bf16[256,256]{0,1:T(8,128)(2,1)}, bf16[256,256]{0,1:T(8,128)(2,1)S(1)}, u32[]{:S(2)}) copy-start(bf16[256,256]{0,1:T(8,128)(2,1)S(1)} %collective-permute-done.3) | copy-start | bytes 393220
  38.2 6.4 %collective-permute-start.4 = (bf16[256,256]{0,1:T(8,128)(2,1)S(1)}, bf16[256,256]{0,1:T(8,128)(2,1)S(1)}, u32[]{:S(2)}, u32[]{:S(2)}) collective-permute-start(bf16[256,256]{0,1:T(8,128)(2,1)S(1)} %collective-permute-done.3), channel_id=1, source_target_pairs={{0,1},{1,2},{2,3},{3,4},{4,5},{5,6},{6,7},{7,8},{8,9},{9,10},{10,1... | collective-permute-start | bytes 393224 | tf_op jit(solution)/shard_map/ppermute | solution.py:17
  44.6 16.0 %copy-start.21 = (bf16[256,256]{0,1:T(8,128)(2,1)}, bf16[256,256]{0,1:T(8,128)(2,1)S(1)}, u32[]{:S(2)}) copy-start(bf16[256,256]{0,1:T(8,128)(2,1)S(1)} %collective-permute-done.4) | copy-start | bytes 393220
  44.6 6.3 %collective-permute-start.5 = (bf16[256,256]{0,1:T(8,128)(2,1)S(1)}, bf16[256,256]{0,1:T(8,128)(2,1)S(1)}, u32[]{:S(2)}, u32[]{:S(2)}) collective-permute-start(bf16[256,256]{0,1:T(8,128)(2,1)S(1)} %collective-permute-done.4), channel_id=1, source_target_pairs={{0,1},{1,2},{2,3},{3,4},{4,5},{5,6},{6,7},{7,8},{8,9},{9,10},{10,1... | collective-permute-start | bytes 393224 | tf_op jit(solution)/shard_map/ppermute | solution.py:17
  50.9 3.2 %copy-start.25 = (bf16[256,256]{0,1:T(8,128)(2,1)}, bf16[256,256]{0,1:T(8,128)(2,1)S(1)}, u32[]{:S(2)}) copy-start(bf16[256,256]{0,1:T(8,128)(2,1)S(1)} %collective-permute-done.5) | copy-start | bytes 393220
  50.9 6.3 %collective-permute-start.6 = (bf16[256,256]{0,1:T(8,128)(2,1)S(1)}, bf16[256,256]{0,1:T(8,128)(2,1)S(1)}, u32[]{:S(2)}, u32[]{:S(2)}) collective-permute-start(bf16[256,256]{0,1:T(8,128)(2,1)S(1)} %collective-permute-done.5), channel_id=1, source_target_pairs={{0,1},{1,2},{2,3},{3,4},{4,5},{5,6},{6,7},{7,8},{8,9},{9,10},{10,1... | collective-permute-start | bytes 393224 | tf_op jit(solution)/shard_map/ppermute | solution.py:17
  57.2 7.0 %copy-start.27 = (bf16[256,256]{0,1:T(8,128)(2,1)}, bf16[256,256]{0,1:T(8,128)(2,1)S(1)}, u32[]{:S(2)}) copy-start(bf16[256,256]{0,1:T(8,128)(2,1)S(1)} %collective-permute-done.6) | copy-start | bytes 393220
  57.2 7.0 %collective-permute-start.7 = (bf16[256,256]{0,1:T(8,128)(2,1)S(1)}, bf16[256,256]{0,1:T(8,128)(2,1)S(1)}, u32[]{:S(2)}, u32[]{:S(2)}) collective-permute-start(bf16[256,256]{0,1:T(8,128)(2,1)S(1)} %collective-permute-done.6), channel_id=1, source_target_pairs={{0,1},{1,2},{2,3},{3,4},{4,5},{5,6},{6,7},{7,8},{8,9},{9,10},{10,1... | collective-permute-start | bytes 393224 | tf_op jit(solution)/shard_map/ppermute | solution.py:17
  99.8 2.5 %copy-start.3 = (f32[768,256]{0,1:T(8,128)S(1)}, f32[768,256]{0,1:T(8,128)}, u32[]{:S(2)}) copy-start(f32[768,256]{0,1:T(8,128)} %get-tuple-element.214) | copy-start | bytes 2359300
  99.9 2.5 %copy-start.8 = (f32[768,256]{0,1:T(8,128)S(1)}, f32[768,256]{0,1:T(8,128)}, u32[]{:S(2)}) copy-start(f32[768,256]{0,1:T(8,128)} %get-tuple-element.206) | copy-start | bytes 2359300
  99.9 2.5 %copy-start.9 = (f32[768,256]{0,1:T(8,128)S(1)}, f32[768,256]{0,1:T(8,128)}, u32[]{:S(2)}) copy-start(f32[768,256]{0,1:T(8,128)} %get-tuple-element.204) | copy-start | bytes 2359300
  102.3 1.4 copy-start.6
  102.3 1.6 copy-start.7
  105.3 2.1 copy-start.16
  105.9 2.0 copy-start.18
  109.7 1.2 copy-start.5
  110.9 1.3 copy-start.2
  112.2 1.5 copy-start.11
  112.2 2.1 copy-start.12
  112.2 2.8 %copy-start.13 = (f32[256,4]{0,1:T(4,128)S(1)}, f32[256,4]{0,1:T(4,128)}, u32[]{:S(2)}) copy-start(f32[256,4]{0,1:T(4,128)} %param.24) | copy-start | bytes 12292
  (8 other events, 9.0 us)
Sparse Core Ops, SparseCore 0:
  10.1 79.0 all-gather.2
  113.8 23.4 reduce-scatter.1

commit v2 on v1

--- a/solution.py
+++ b/solution.py
@@ -1,6 +1,7 @@
 import functools
 import jax
 import jax.numpy as jnp
+import numpy as np
 from jax import lax
 from jax.experimental import pallas as pl
 from jax.experimental.pallas import tpu as pltpu
@@ -8,80 +9,6 @@
 
 KVH = 2
 HD = 128
-TOPK = 4
-
-
-def passed_along(value, axis, by):
-    devices = lax.axis_size(axis)
-    pairs = [(i, i + by) for i in range(devices) if 0 <= i + by < devices]
-    return lax.ppermute(value, axis, pairs)
-
-
-def rms_norm(values, gain):
-    wide = values.astype(jnp.float32)
-    return wide * lax.rsqrt(jnp.mean(wide * wide, axis=-1, keepdims=True) + 1e-05) * gain
-
-
-def rotate(vectors, positions):
-    half = vectors.shape[-1] // 2
-    freqs = 10000.0 ** (-2.0 * jnp.arange(half, dtype=jnp.float32) / vectors.shape[-1])
-    angle = positions[:, None] * freqs[None, :]
-    cosine = jnp.cos(angle)[:, None, :]
-    sine = jnp.sin(angle)[:, None, :]
-    first = vectors[..., :half]
-    second = vectors[..., half:]
-    return jnp.concatenate(
-        [first * cosine - second * sine, second * cosine + first * sine], axis=-1
-    )
-
-
-def request_info(index, lengths):
-    ends = jnp.cumsum(lengths)
-    seg = jnp.sum((index[:, None] >= ends[None, :]).astype(jnp.int32), axis=1)
-    starts = ends - lengths
-    count = lengths.shape[0]
-    begin = jnp.sum(
-        jnp.where(seg[:, None] == jnp.arange(count, dtype=jnp.int32)[None, :], starts[None, :], 0),
-        axis=1,
-    )
-    return (seg, index - begin)
-
-
-def matmul(left, right):
-    return jnp.dot(left, right, preferred_element_type=jnp.float32)
-
-
-def attend(state, queries, piece, valid):
-    best, total, accum = state
-    keys = piece[:, :HD]
-    values = piece[:, HD:]
-    scores = lax.dot_general(
-        queries, keys, (((1,), (1,)), ((), ())), preferred_element_type=jnp.float32
-    )
-    if valid is not None:
-        scores = jnp.where(valid, scores, -1e30)
-    new_best = jnp.maximum(best, jnp.max(scores, axis=1))
-    weights = jnp.exp(scores - new_best[:, None])
-    if valid is not None:
-        weights = jnp.where(valid, weights, 0.0)
-    rescale = jnp.exp(best - new_best)
-    total = total * rescale + jnp.sum(weights, axis=1)
-    accum = accum * rescale[:, None] + matmul(weights.astype(jnp.bfloat16), values)
-    return (new_best, total, accum)
-
-
-def attend_blocks(state, queries, piece, key_start, masker):
-    count = piece.shape[0]
-    width = 2048 if count > 2048 and count % 2048 == 0 else count
-
-    def one_part(number, current):
-        part = lax.dynamic_slice_in_dim(piece, number * width, width, 0)
-        valid = masker(key_start + number * width, width) if masker is not None else None
-        return attend(current, queries, part, valid)
-
-    if width == count:
-        return one_part(0, state)
-    return lax.fori_loop(0, count // width, one_part, state)
 
 
 MESH = pl.DeviceIdType.MESH
@@ -497,6 +424,440 @@
     return out.reshape(xs * count, width // xs)
 
 
+PAST = 4
+SPLIT = 5
+
+
+def attention_kernel(
+    sizes,
+    lengths_ref,
+    hidden_ref,
+    gain_ref,
+    freqs_ref,
+    w_query_ref,
+    w_keyval_ref,
+    prefix_ref,
+    w_out_ref,
+    mid_ref,
+    w_kv,
+    cached,
+    fresh,
+    out_weights,
+    query,
+    begin,
+    best,
+    total,
+    accum,
+    context,
+    contexts,
+    local_sem,
+    pz_send,
+    pz_recv,
+    py_send,
+    py_recv,
+    pc_send,
+    pc_recv,
+    nz_send,
+    nz_recv,
+    nc_send,
+    nc_recv,
+    wx_send,
+    wx_recv,
+    wc_send,
+    wc_recv,
+    cx_send,
+    cx_recv,
+):
+    xs, ys, zs = sizes
+    head = lax.axis_index("head")
+    blk = lax.axis_index("blk")
+    core = blk % CORES
+    chip = blk // CORES
+    z = chip % zs
+    y = chip // zs
+    count, width = hidden_ref.shape
+    heads = query.shape[0]
+    part = count // xs
+    half = w_out_ref.shape[0] // CORES
+
+    def at(dx=0, dy=0, dz=0, other=False):
+        cc = 1 - core if other else core
+        return (
+            (head + dx) % xs,
+            (((y + dy) % ys) * zs + (z + dz) % zs) * CORES + cc,
+        )
+
+    def along(step):
+        return (head, ((chip + step) % (ys * zs)) * CORES + core)
+
+    peers = (
+        [at(other=True), at(dz=1), at(dz=zs - 1), at(dy=1), at(dy=ys - 1)]
+        + [at(dx=d) for d in range(1, xs)]
+        + [along(1), along(ys * zs - 1)]
+    )
+    barrier = pltpu.get_barrier_semaphore()
+    for peer in peers:
+        pl.semaphore_signal(barrier, inc=1, device_id=peer, device_id_type=MESH)
+
+    def remote(source, target, send, recv, device):
+        return pltpu.make_async_remote_copy(
+            src_ref=source,
+            dst_ref=target,
+            send_sem=send,
+            recv_sem=recv,
+            device_id=device,
+            device_id_type=MESH,
+        )
+
+    kv_copy = pltpu.make_async_copy(w_keyval_ref.at[head // (xs // KVH)], w_kv, local_sem.at[0])
+    kv_copy.start()
+    out_copy = pltpu.make_async_copy(w_out_ref, out_weights.at[0], local_sem.at[1])
+    out_copy.start()
+    cached[0, 0, 0] = prefix_ref[...]
+    pl.semaphore_wait(barrier, len(peers))
+
+    sent = []
+
+    def go(copy):
+        copy.start()
+        sent.append(copy)
+        return copy
+
+    def prefix_z(direction, step):
+        held = (-step * direction) % zs
+        there = (held - direction) % zs
+        side = 0 if direction == 1 else 1
+        return remote(
+            cached.at[0, 0, PLACE[held]],
+            cached.at[0, 0, PLACE[there]],
+            pz_send.at[side, step],
+            pz_recv.at[side, step],
+            at(dz=direction),
+        )
+
+    batches = (pl.ds(0, SPLIT), pl.ds(SPLIT, zs - SPLIT))
+
+    def prefix_y(held, direction, batch):
+        there = (held - direction) % ys
+        return remote(
+            cached.at[0, held, batches[batch]],
+            cached.at[0, there, batches[batch]],
+            py_send.at[there, batch],
+            py_recv.at[there, batch],
+            at(dy=direction),
+        )
+
+    def prefix_core(held, batch):
+        return remote(
+            cached.at[0, held, batches[batch]],
+            cached.at[1, held, batches[batch]],
+            pc_send.at[held, batch],
+            pc_recv.at[held, batch],
+            at(other=True),
+        )
+
+    flow = {}
+    flow[1, 0] = go(prefix_z(1, 0))
+    flow[-1, 0] = go(prefix_z(-1, 0))
+
+    mine = pl.ds(pl.multiple_of(core * half, 64), half)
+
+    def weights_x(held, direction):
+        there = (held - direction) % xs
+        rows = mine
+        if held != 0:
+            offset = 0 if direction == 1 else half // 2
+            rows = pl.ds(pl.multiple_of(core * half + offset, 32), half // 2)
+        number = there if held == 0 else (0 if direction == 1 else 2)
+        source = w_out_ref.at[rows] if held == 0 else out_weights.at[held, rows]
+        return remote(
+            source,
+            out_weights.at[there, rows],
+            wx_send.at[number],
+            wx_recv.at[number],
+            at(dx=direction),
+        )
+
+    def weights_core(held):
+        return remote(
+            out_weights.at[held, mine],
+            out_weights.at[held, mine],
+            wc_send.at[held],
+            wc_recv.at[held],
+            at(other=True),
+        )
+
+    go(weights_x(0, 1))
+    go(weights_x(0, -1))
+
+    token = blk * count + lax.broadcasted_iota(jnp.int32, (count, HD), 0)
+    start = jnp.zeros((count, HD), jnp.int32)
+    end = jnp.int32(0)
+    for r in range(lengths_ref.shape[0]):
+        end = end + lengths_ref[r]
+        start = jnp.where(token >= end, end, start)
+    begin[...] = start
+    prefix_total = cached.shape[0] * ys * zs * prefix_ref.shape[0]
+    angle = (prefix_total + token - start).astype(jnp.float32) * freqs_ref[...]
+    cosine = jnp.cos(angle)
+    sine = jnp.sin(angle)
+    lane = lax.broadcasted_iota(jnp.int32, (count, HD), 1)
+    sine = jnp.where(lane < HD // 2, -sine, sine)
+
+    def turned(vectors):
+        return vectors * cosine + pltpu.roll(vectors, HD // 2, 1) * sine
+
+    wide = hidden_ref[...].astype(jnp.float32)
+    scale = lax.rsqrt(jnp.mean(wide * wide, axis=-1, keepdims=True) + 1e-05)
+    normed = (wide * scale * gain_ref[...]).astype(jnp.bfloat16)
+    kv_copy.wait()
+    keyval = jnp.dot(normed, w_kv[...], preferred_element_type=jnp.float32)
+    fresh[0, 0, 0] = turned(keyval[:, :HD]).astype(jnp.bfloat16)
+    fresh[0, 1, 0] = keyval[:, HD:].astype(jnp.bfloat16)
+
+    def fresh_next(distance, kind):
+        return remote(
+            fresh.at[distance, kind, 0],
+            fresh.at[distance + 1, kind, 0],
+            nz_send.at[distance, kind],
+            nz_recv.at[distance, kind],
+            along(1),
+        )
+
+    def fresh_core(distance, kind):
+        return remote(
+            fresh.at[distance, kind, 0],
+            fresh.at[distance, kind, 1],
+            nc_send.at[distance, kind],
+            nc_recv.at[distance, kind],
+            at(other=True),
+        )
+
+    chain = {}
+    shared = {}
+    for kind in range(2):
+        chain[0, kind] = go(fresh_next(0, kind))
+    for kind in range(2):
+        shared[0, kind] = go(fresh_core(0, kind))
+
+    def prefix_step(step):
+        for direction in (1, -1):
+            if (direction, step - 1) in flow:
+                flow[direction, step - 1].wait_recv()
+            if step < zs // 2 - (0 if direction == 1 else 1):
+                flow[direction, step] = go(prefix_z(direction, step))
+
+    def fresh_step(distance):
+        for kind in range(2):
+            chain[distance - 1, kind].wait_recv()
+            if distance < PAST:
+                chain[distance, kind] = go(fresh_next(distance, kind))
+            shared[distance, kind] = go(fresh_core(distance, kind))
+
+    prefix_step(1)
+    queries = jnp.dot(normed, w_query_ref[...], preferred_element_type=jnp.float32)
+    for j in range(heads):
+        query[j] = (turned(queries[:, j * HD : (j + 1) * HD]) * HD ** (-0.5)).astype(jnp.bfloat16)
+    best[...] = jnp.full(best.shape, -1e30, jnp.float32)
+    total[...] = jnp.zeros(total.shape, jnp.float32)
+    accum[...] = jnp.zeros(accum.shape, jnp.float32)
+
+    def attend(keys, values, distance=None):
+        length = keys.shape[0]
+        if distance is not None:
+            place = lax.broadcasted_iota(jnp.int32, (1, length), 1)
+            own_block = (blk - CORES * distance) * count
+            other_block = (blk + 1 - 2 * core - CORES * distance) * count
+            where = jnp.where(place < count, own_block + place, other_block + place - count)
+
+        def one_head(j, carry):
+            scores = lax.dot_general(
+                query[j], keys, (((1,), (1,)), ((), ())), preferred_element_type=jnp.float32
+            )
+            if distance is not None:
+                valid = where >= begin[:, :1]
+                if distance == 0:
+                    row = blk * count + lax.broadcasted_iota(jnp.int32, (count, 1), 0)
+                    valid = valid & (where <= row)
+                scores = jnp.where(valid, scores, -1e30)
+            old = best[j]
+            new = jnp.maximum(old, jnp.max(scores, axis=1, keepdims=True))
+            weights = jnp.exp(scores - new[:, :1])
+            rescale = jnp.exp(old - new)
+            best[j] = new
+            total[j] = total[j] * rescale + jnp.sum(weights, axis=1, keepdims=True)
+            accum[j] = accum[j] * rescale + jnp.dot(
+                weights.astype(jnp.bfloat16), values, preferred_element_type=jnp.float32
+            )
+            return carry
+
+        lax.fori_loop(0, heads, one_head, 0)
+
+    def attend_fresh(distance):
+        for kind in range(2):
+            shared[distance, kind].wait_recv()
+        attend(
+            fresh[distance, 0].reshape(CORES * count, HD),
+            fresh[distance, 1].reshape(CORES * count, HD),
+            distance,
+        )
+
+    def attend_cached(side, held):
+        piece = cached[side, held].reshape(zs * prefix_ref.shape[0], 2 * HD)
+        attend(piece[:, :HD], piece[:, HD:])
+
+    ride = {}
+    onchip = {}
+
+    def prefix_share(held, batch):
+        onchip[held, batch] = go(prefix_core(held, batch))
+
+    def prefix_row(batch):
+        for direction in (1, -1):
+            ride[(-direction) % ys, batch] = go(prefix_y(0, direction, batch))
+        prefix_share(0, batch)
+
+    def prefix_arrived(batch):
+        ride[ys - 1, batch].wait_recv()
+        if batch == 0:
+            ride[2, batch] = go(prefix_y(ys - 1, 1, batch))
+        ride[1, batch].wait_recv()
+        if batch == 1:
+            ride[2, batch] = go(prefix_y(1, -1, batch))
+        prefix_share(ys - 1, batch)
+        prefix_share(1, batch)
+
+    def other_side(held):
+        for batch in range(2):
+            onchip[held, batch].wait_recv()
+
+    prefix_step(2)
+    prefix_row(0)
+    attend_fresh(0)
+    prefix_step(3)
+    fresh_step(1)
+    prefix_step(4)
+    prefix_row(1)
+    attend_cached(0, 0)
+    prefix_arrived(0)
+    other_side(0)
+    attend_cached(1, 0)
+    fresh_step(2)
+    prefix_arrived(1)
+    attend_fresh(1)
+    attend_cached(0, ys - 1)
+    fresh_step(3)
+    attend_cached(0, 1)
+    ride[2, 0].wait_recv()
+    prefix_share(2, 0)
+    ride[2, 1].wait_recv()
+    prefix_share(2, 1)
+    attend_fresh(2)
+    fresh_step(4)
+    other_side(ys - 1)
+    attend_cached(1, ys - 1)
+    out_ring = {3: weights_x(0, 1), 1: weights_x(0, -1)}
+    out_ring[3].wait_recv()
+    relay_right = go(weights_x(3, 1))
+    out_ring[1].wait_recv()
+    relay_left = go(weights_x(1, -1))
+    out_shared = {held: go(weights_core(held)) for held in (3, 1)}
+    other_side(1)
+    attend_cached(1, 1)
+    attend_cached(0, 2)
+    attend_fresh(3)
+    other_side(2)
+    attend_cached(1, 2)
+    attend_fresh(4)
+
+    for j in range(heads):
+        value = (accum[j] / total[j]).astype(jnp.bfloat16)
+        context[:, :, j * HD : (j + 1) * HD] = value.reshape(xs, part, HD)
+    crossing = {}
+    for dx in (2, 1, 3):
+        crossing[xs - dx] = go(
+            remote(
+                context.at[(head + dx) % xs],
+                contexts.at[xs - dx],
+                cx_send.at[dx],
+                cx_recv.at[xs - dx],
+                at(dx=dx),
+            )
+        )
+    contexts[0] = context[head]
+    relay_right.wait_recv()
+    relay_left.wait_recv()
+    out_shared[2] = go(weights_core(2))
+    out_copy.wait()
+
+    def term(held):
+        return jnp.dot(contexts[held], out_weights[held], preferred_element_type=jnp.float32)
+
+    value = hidden_ref[pl.ds(pl.multiple_of(head * part, part), part)].astype(jnp.float32)
+    attn = term(0)
+    for held in (3, 1, 2):
+        out_shared[held].wait_recv()
+        crossing[held].wait_recv()
+        attn = attn + term(held)
+    mid_ref[...] = (value + attn).astype(jnp.bfloat16)
+    for copy in sent:
+        copy.wait_send()
+
+
+def attention(sizes, hidden, gain, w_query, w_keyval, prefix, w_out, lengths):
+    xs, ys, zs = sizes
+    count, width = hidden.shape
+    heads = w_query.shape[1] // HD
+    columns = w_query.shape[1]
+    bf16, f32 = jnp.bfloat16, jnp.float32
+    half = np.arange(HD // 2, dtype=np.float32)
+    freqs = (10000.0 ** (-2.0 * half / HD)).astype(np.float32)
+    freqs = jnp.asarray(np.concatenate([freqs, freqs])[None, :])
+    dma = pltpu.SemaphoreType.DMA
+    vmem = pl.BlockSpec(memory_space=pltpu.VMEM)
+    smem = pl.BlockSpec(memory_space=pltpu.SMEM)
+    hbm = pl.BlockSpec(memory_space=pl.ANY)
+    return pl.pallas_call(
+        functools.partial(attention_kernel, sizes),
+        out_shape=jax.ShapeDtypeStruct((count // xs, width), bf16),
+        in_specs=[smem, vmem, vmem, vmem, vmem, hbm, vmem, hbm],
+        out_specs=vmem,
+        scratch_shapes=[
+            pltpu.VMEM(w_keyval.shape[1:], bf16),
+            pltpu.VMEM((CORES, ys, zs) + prefix.shape, bf16),
+            pltpu.VMEM((PAST + 1, 2, CORES, count, HD), bf16),
+            pltpu.VMEM((xs,) + w_out.shape, bf16),
+            pltpu.VMEM((heads, count, HD), bf16),
+            pltpu.VMEM((count, HD), jnp.int32),
+            pltpu.VMEM((heads, count, HD), f32),
+            pltpu.VMEM((heads, count, HD), f32),
+            pltpu.VMEM((heads, count, HD), f32),
+            pltpu.VMEM((xs, count // xs, columns), bf16),
+            pltpu.VMEM((xs, count // xs, columns), bf16),
+            dma((2,)),
+            dma((2, zs // 2)),
+            dma((2, zs // 2)),
+            dma((ys, 2)),
+            dma((ys, 2)),
+            dma((ys, 2)),
+            dma((ys, 2)),
+            dma((PAST, 2)),
+            dma((PAST, 2)),
+            dma((PAST + 1, 2)),
+            dma((PAST + 1, 2)),
+            dma((xs,)),
+            dma((xs,)),
+            dma((xs,)),
+            dma((xs,)),
+            dma((xs,)),
+            dma((xs,)),
+        ],
+        compiler_params=pltpu.CompilerParams(
+            collective_id=0, has_side_effects=True, vmem_limit_bytes=60 * 2**20
+        ),
+    )(lengths, hidden, gain.reshape(1, width), freqs, w_query, w_keyval, prefix, w_out)
+
+
 def shards(
     hidden_in,
     attn_gain,
@@ -511,70 +872,19 @@
     route_weights,
     lengths,
 ):
-    tok_rows = hidden_in.shape[0]
     head_index = lax.axis_index("head")
-    block_index = lax.axis_index("blk")
     head_count = lax.axis_size("head")
     block_count = lax.axis_size("blk")
-    local_heads = w_query.shape[1] // HD
+    quarter = hidden_in.shape[0] // head_count
+    chips_z = 8
+    sizes = (head_count, block_count // (CORES * chips_z), chips_z)
     kv_head = head_index // (head_count // KVH)
-    prefix_total = prefix_cache.shape[0] * block_count
-    normed = rms_norm(hidden_in, attn_gain).astype(jnp.bfloat16)
-    token_index = block_index * tok_rows + jnp.arange(tok_rows, dtype=jnp.int32)
-    seg_query, offset_query = request_info(token_index, lengths)
-    positions = (prefix_total + offset_query).astype(jnp.float32)
-    queries = matmul(normed, w_query).reshape(tok_rows, local_heads, HD)
-    queries = (
-        (rotate(queries, positions) * HD ** (-0.5))
-        .astype(jnp.bfloat16)
-        .reshape(tok_rows * local_heads, HD)
+    cached = lax.dynamic_index_in_dim(prefix_cache, kv_head, 1, keepdims=False)
+    middle = attention(
+        sizes, hidden_in, attn_gain, w_query, w_keyval, cached, w_out, lengths
     )
-    own_weights = lax.dynamic_index_in_dim(w_keyval, kv_head, 0, keepdims=False)
-    keyval = matmul(normed, own_weights)
-    new_keys = rotate(keyval[:, None, :HD], positions)[:, 0, :]
-    own_block = jnp.concatenate([new_keys, keyval[:, HD:]], axis=1).astype(jnp.bfloat16)
-    cached = lax.dynamic_index_in_dim(prefix_cache, kv_head, 1, keepdims=False)
-    row_index = jnp.repeat(token_index, local_heads)
-    row_seg = jnp.repeat(seg_query, local_heads)
-    row_total = tok_rows * local_heads
-
-    def suffix_mask(key_start, count):
-        key_index = key_start + jnp.arange(count, dtype=jnp.int32)
-        key_seg, unused = request_info(key_index, lengths)
-        return (
-            (row_seg[:, None] == key_seg[None, :])
-            & (key_index[None, :] <= row_index[:, None])
-            & (key_index[None, :] >= 0)
-        )
-
-    state = (
-        jnp.full((row_total,), -1e30, jnp.float32),
-        jnp.zeros((row_total,), jnp.float32),
-        jnp.zeros((row_total, HD), jnp.float32),
-    )
-    state = attend_blocks(
-        state, queries, lax.all_gather(cached, "blk", axis=0, tiled=True), jnp.int32(0), None
-    )
-    state = attend_blocks(state, queries, own_block, block_index * tok_rows, suffix_mask)
-    travelling = own_block
-    reach = min(8, block_count // 2)
-    for distance in range(reach):
-        travelling = passed_along(travelling, "blk", 1)
-        state = attend_blocks(
-            state, queries, travelling, (block_index - distance - 1) * tok_rows, suffix_mask
-        )
-    best, total, accum = state
-    context = (accum / total[:, None]).astype(jnp.bfloat16).reshape(tok_rows, local_heads * HD)
-    quarter = tok_rows // head_count
-    attn_share = lax.psum_scatter(
-        matmul(context, w_out).astype(jnp.bfloat16), "head", scatter_dimension=0, tiled=True
-    ).astype(jnp.float32)
-    resid = lax.dynamic_slice_in_dim(hidden_in, head_index * quarter, quarter, 0)
-    middle = (resid.astype(jnp.float32) + attn_share).astype(jnp.bfloat16)
     my_routes = lax.dynamic_slice_in_dim(routes, head_index * quarter, quarter, 0)
     my_weights = lax.dynamic_slice_in_dim(route_weights, head_index * quarter, quarter, 0)
-    chips_z = 8
-    sizes = (head_count, block_count // (CORES * chips_z), chips_z)
     return moe(sizes, middle, moe_gain, my_routes, my_weights, w_gateup, w_down)
 
 

time: 221 us -> 133 us (0.60)
  waiting for transfers between devices: 64.9 us -> 0 us
  Pallas kernels: 72.6 us -> 125 us
  matrix products: 31.1 us -> 0 us
  starting transfers between devices: 17.5 us -> 0 us
  between operations: 14.2 us -> 0.03 us
  other arithmetic: 11.2 us -> 0 us
    pallas_call x0 -> x1, Pallas kernels: none -> 54.4 us  [attention(): pl.pallas_call(functools.partial(attention_kernel, sizes), out_shape=jax....]
    dot_general x25 -> x0, matrix products: 31.1 us -> none  [the longest x14 15.7 us: matmul(): return jnp.dot(left, right, preferred_element_type=jnp.float32)]
    all_gather x1 -> x0, waiting for transfers between devices: 23.2 us -> none  [shards(): lax.all_gather(cached, 'blk', axis=0, tiled=True)]
    reduce_scatter x1 -> x0, waiting for transfers between devices: 21.7 us -> none  [shards(): lax.psum_scatter(matmul(context, w_out).astype(jnp.bfloat16), 'head', sca...]
    ppermute x8 -> x0, waiting for transfers between devices: 20 us -> none  [passed_along(): return lax.ppermute(value, axis, pairs)]
    ppermute x8 -> x0, starting transfers between devices: 17.5 us -> none  [passed_along(): return lax.ppermute(value, axis, pairs)]
    reduce_sum x8 -> x0, other arithmetic: 8.2 us -> none  [the longest x5 6.61 us: attend(): total = total * rescale + jnp.sum(weights, axis=1)]
  transfers between devices with their start and end apart: 10 -> 0, of which waited for: 9 -> 0; matrix products, arithmetic and copies ran while one was open for 10% -> 0% of each run, Pallas kernels for 0% -> 0%
where the time goes in v2:
time: 133 us
  Pallas kernels  125 us (94%)
  local copies, waits for them, and re-layouts  7.62 us (6%)
    pallas_call x1, Pallas kernels, moe(): pl.pallas_call(functools.partial(moe_kernel, sizes), out_shape=jax.ShapeD...  70.8 us
    pallas_call x1, Pallas kernels, attention(): pl.pallas_call(functools.partial(attention_kernel, sizes), out_shape=jax....  54.4 us

profile of v2, /device:TPU:32, one launch (start us, length us, event | category | flops | bytes accessed | tf_op | source)
XLA Modules:
  0.0 132.9 jit_solution(14084780822685411311)
XLA Ops:
  0.0 0.0 copy-start
  0.0 0.8 constant_dynamic-slice_fusion.1
  0.8 0.6 pad_bitcast_fusion.1.routes_ref
  1.4 0.8 constant_dynamic-slice_fusion
  2.1 0.6 pad_bitcast_fusion.weights_ref
  2.7 1.3 reshape.9.gain_ref
  4.0 1.3 reshape.10.gain_ref
  5.3 0.0 copy-done
  5.3 0.1 constant_dynamic-slice_fusion.2
  5.4 0.6 copy.17
  6.0 54.4 %shard_map.127.mid_ref = bf16[64,1536]{1,0:T(8,128)(2,1)} custom-call(s32[32]{0:T(128)} %lengths_ref.1, bf16[256,1536]{1,0:T(8,128)(2,1)} %hidden_ref.1, f32[1,1536]{1,0:T(1,128)} %reshape.9.gain_ref, f32[1,128]{1,0:T(1,128)} %constant.35.clone.freqs_ref, bf16[1536,384]{1,0:T(8,128)(2,1)} %w_query_ref.1, bf16[2,1536,256]{2,1,0:T(8,128)(2,1)} %w_keyval_ref.1, ...), custom_call_target="tpu_custom_call" | custom-call | tf_op jit(solution)/shard_map/pallas_call | solution.py:820
  60.4 70.8 %shard_map.128 = bf16[4,64,384]{2,1,0:T(8,128)(2,1)} custom-call(bf16[64,1536]{1,0:T(8,128)(2,1)} %shard_map.127.mid_ref, f32[1,1536]{1,0:T(1,128)} %reshape.10.gain_ref, s32[4,128]{1,0:T(4,128)} %pad_bitcast_fusion.1.routes_ref, f32[4,128]{1,0:T(4,128)} %pad_bitcast_fusion.weights_ref, bf16[1,1536,768]{2,1,0:T(8,128)(2,1)} %gateup_ref.1, ...), custom_call_target="tpu_custom_call" | custom-call | tf_op jit(solution)/shard_map/pallas_call | solution.py:382
  131.3 1.6 %copy.19 = bf16[256,384]{1,0:T(8,128)(2,1)} copy(bf16[256,384]{1,0:T(8,128)(2,1)} %bitcast.8) | data formatting | bytes 393216
Async XLA Ops:
  0.0 5.3 %copy-start = (bf16[64,2,256]{2,1,0:T(2,128)(2,1)S(1)}, bf16[64,2,256]{2,1,0:T(2,128)(2,1)}, u32[]{:S(2)}) copy-start(bf16[64,2,256]{2,1,0:T(2,128)(2,1)} %param.17) | copy-start | bytes 196612

commit v3 on v1

v3 whole, which is shorter than its diff:
```python
import functools
import jax
import jax.numpy as jnp
import numpy as np
from jax import lax
from jax.experimental import pallas as pl
from jax.experimental.pallas import tpu as pltpu
from jax.sharding import PartitionSpec as P

KVH = 2
HD = 128
PAST = 4
SPLIT = 4
MESH = pl.DeviceIdType.MESH
CORES = 2
ROWS_BLOCK = 64
PIECE = 16
ORDER = (0, 7, 1, 6, 2, 5, 3, 4)
PLACE = {rel: at for at, rel in enumerate(ORDER)}


def layer_kernel(
    sizes,
    lengths_ref,
    hidden_ref,
    gain_ref,
    freqs_ref,
    w_query_ref,
    w_keyval_ref,
    prefix_ref,
    w_out_ref,
    moe_gain_ref,
    routes_ref,
    weights_ref,
    gateup_ref,
    down_ref,
    out_ref,
    w_kv,
    cached,
    fresh,
    out_weights,
    query,
    begin,
    best,
    total,
    accum,
    context,
    contexts,
    mid_ref,
    tokens,
    table,
    tables,
    packed,
    rows,
    outs,
    backs,
    way_out,
    way_back,
    gate_up,
    down,
    partial,
    sums_r,
    sums_l,
    got_r,
    got_l,
    final,
    landed,
    local_sem,
    pz_send,
    pz_recv,
    py_send,
    py_recv,
    pc_send,
    pc_recv,
    nz_send,
    nz_recv,
    nc_send,
    nc_recv,
    wx_send,
    wx_recv,
    wc_send,
    wc_recv,
    cx_send,
    cx_recv,
    ws_send,
    ws_recv,
    tsend,
    trecv,
    zsend,
    zrecv,
    ysend,
    yrecv,
    bsend,
    brecv,
    vsend,
    vrecv,
    ssend,
    srecv,
    xsend,
    xrecv,
):
    xs, ys, zs = sizes
    head = lax.axis_index("head")
    blk = lax.axis_index("blk")
    core = blk % CORES
    chip = blk // CORES
    z = chip % zs
    y = chip // zs
    count, width = hidden_ref.shape
    heads = query.shape[0]
    part = count // xs
    half = w_out_ref.shape[0] // CORES

    def at(dx=0, dy=0, dz=0, other=False):
        cc = 1 - core if other else core
        return (
            (head + dx) % xs,
            (((y + dy) % ys) * zs + (z + dz) % zs) * CORES + cc,
        )

    def along(step):
        return (head, ((chip + step) % (ys * zs)) * CORES + core)

    peers = (
        [at(other=True)]
        + [at(dz=d) for d in range(1, zs)]
        + [at(dy=d) for d in range(1, ys)]
        + [at(dx=d) for d in range(1, xs)]
        + [along(1), along(ys * zs - 1)]
    )
    barrier = pltpu.get_barrier_semaphore()
    for peer in peers:
        pl.semaphore_signal(barrier, inc=1, device_id=peer, device_id_type=MESH)

    def remote(source, target, send, recv, device):
        return pltpu.make_async_remote_copy(
            src_ref=source,
            dst_ref=target,
            send_sem=send,
            recv_sem=recv,
            device_id=device,
            device_id_type=MESH,
        )

    kv_copy = pltpu.make_async_copy(w_keyval_ref.at[head // (xs // KVH)], w_kv, local_sem.at[0])
    kv_copy.start()
    out_copy = pltpu.make_async_copy(w_out_ref, out_weights.at[0], local_sem.at[1])
    out_copy.start()
    own_copies = [
        pltpu.make_async_copy(gateup_ref.at[0], gate_up.at[0], local_sem.at[2]),
        pltpu.make_async_copy(down_ref.at[0], down.at[0], local_sem.at[3]),
    ]
    for copy in own_copies:
        copy.start()
    kv_head = head // (xs // KVH)
    piece = prefix_ref[:, 0, :]
    for g in range(1, KVH):
        piece = jnp.where(kv_head == g, prefix_ref[:, g, :], piece)
    cached[0, 0, 0] = piece
    pl.semaphore_wait(barrier, len(peers))

    sent = []

    def go(copy):
        copy.start()
        sent.append(copy)
        return copy

    def prefix_z(direction, step):
        held = (-step * direction) % zs
        there = (held - direction) % zs
        side = 0 if direction == 1 else 1
        return remote(
            cached.at[0, 0, PLACE[held]],
            cached.at[0, 0, PLACE[there]],
            pz_send.at[side, step],
            pz_recv.at[side, step],
            at(dz=direction),
        )

    batches = (pl.ds(0, SPLIT), pl.ds(SPLIT, zs - SPLIT))

    def prefix_y(held, direction, batch):
        there = (held - direction) % ys
        return remote(
            cached.at[0, held, batches[batch]],
            cached.at[0, there, batches[batch]],
            py_send.at[there, batch],
            py_recv.at[there, batch],
            at(dy=direction),
        )

    def prefix_core(held, batch):
        return remote(
            cached.at[0, held, batches[batch]],
            cached.at[1, held, batches[batch]],
            pc_send.at[held, batch],
            pc_recv.at[held, batch],
            at(other=True),
        )

    flow = {}
    flow[1, 0] = go(prefix_z(1, 0))
    flow[-1, 0] = go(prefix_z(-1, 0))

    mine = pl.ds(pl.multiple_of(core * half, 64), half)

    def weights_x(held, direction):
        there = (held - direction) % xs
        rows = mine
        if held != 0:
            offset = 0 if direction == 1 else half // 2
            rows = pl.ds(pl.multiple_of(core * half + offset, 32), half // 2)
        number = there if held == 0 else (0 if direction == 1 else 2)
        source = w_out_ref.at[rows] if held == 0 else out_weights.at[held, rows]
        return remote(
            source,
            out_weights.at[there, rows],
            wx_send.at[number],
            wx_recv.at[number],
            at(dx=direction),
        )

    def weights_core(held):
        return remote(
            out_weights.at[held, mine],
            out_weights.at[held, mine],
            wc_send.at[held],
            wc_recv.at[held],
            at(other=True),
        )

    out_ring = {3: go(weights_x(0, 1)), 1: go(weights_x(0, -1))}

    token = blk * count + lax.broadcasted_iota(jnp.int32, (count, HD), 0)
    start = jnp.zeros((count, HD), jnp.int32)
    end = jnp.int32(0)
    for r in range(lengths_ref.shape[0]):
        end = end + lengths_ref[r]
        start = jnp.where(token >= end, end, start)
    begin[...] = start
    prefix_total = cached.shape[0] * ys * zs * prefix_ref.shape[0]
    angle = (prefix_total + token - start).astype(jnp.float32) * freqs_ref[...]
    cosine = jnp.cos(angle)
    sine = jnp.sin(angle)
    lane = lax.broadcasted_iota(jnp.int32, (count, HD), 1)
    sine = jnp.where(lane < HD // 2, -sine, sine)

    def turned(vectors):
        return vectors * cosine + pltpu.roll(vectors, HD // 2, 1) * sine

    wide = hidden_ref[...].astype(jnp.float32)
    scale = lax.rsqrt(jnp.mean(wide * wide, axis=-1, keepdims=True) + 1e-05)
    normed = (wide * scale * gain_ref[...].reshape(1, width)).astype(jnp.bfloat16)
    kv_copy.wait()
    keyval = jnp.dot(normed, w_kv[...], preferred_element_type=jnp.float32)
    fresh[0, 0, 0] = turned(keyval[:, :HD]).astype(jnp.bfloat16)
    fresh[0, 1, 0] = keyval[:, HD:].astype(jnp.bfloat16)

    def fresh_next(distance, kind):
        return remote(
            fresh.at[distance, kind, 0],
            fresh.at[distance + 1, kind, 0],
            nz_send.at[distance, kind],
            nz_recv.at[distance, kind],
            along(1),
        )

    def fresh_core(distance, kind):
        return remote(
            fresh.at[distance, kind, 0],
            fresh.at[distance, kind, 1],
            nc_send.at[distance, kind],
            nc_recv.at[distance, kind],
            at(other=True),
        )

    chain = {}
    shared = {}
    for kind in range(2):
        chain[0, kind] = go(fresh_next(0, kind))
    for kind in range(2):
        shared[0, kind] = go(fresh_core(0, kind))

    def prefix_step(step):
        for direction in (1, -1):
            if (direction, step - 1) in flow:
                flow[direction, step - 1].wait_recv()
            if step < zs // 2 - (0 if direction == 1 else 1):
                flow[direction, step] = go(prefix_z(direction, step))

    def fresh_step(distance, kind):
        chain[distance - 1, kind].wait_recv()
        if distance < PAST:
            chain[distance, kind] = go(fresh_next(distance, kind))
        shared[distance, kind] = go(fresh_core(distance, kind))

    prefix_step(1)
    queries = jnp.dot(normed, w_query_ref[...], preferred_element_type=jnp.float32)
    for j in range(heads):
        query[j] = (turned(queries[:, j * HD : (j + 1) * HD]) * HD ** (-0.5)).astype(jnp.bfloat16)
    lanes = table.shape[2]
    wanted = routes_ref[pl.ds(pl.multiple_of(head * part, part), part), :]
    given = weights_ref[pl.ds(pl.multiple_of(head * part, part), part), :]
    column = lax.broadcasted_iota(jnp.int32, (part, lanes), 1)
    group = column % (2 * ys)
    expert = ((y + group % ys) % ys) * zs + column // (2 * ys)
    hit = jnp.zeros((part, lanes), jnp.float32)
    weight = jnp.zeros((part, lanes), jnp.float32)
    for k in range(routes_ref.shape[1]):
        same = wanted[:, k : k + 1] == expert
        hit = hit + jnp.where(same, 1.0, 0.0)
        weight = weight + jnp.where(same, given[:, k : k + 1], 0.0)
    before = jnp.where(
        lax.broadcasted_iota(jnp.int32, (part, part), 1)
        < lax.broadcasted_iota(jnp.int32, (part, part), 0),
        1.0,
        0.0,
    )
    rank = jnp.dot(
        before.astype(jnp.bfloat16),
        hit.astype(jnp.bfloat16),
        preferred_element_type=jnp.float32,
    )
    code = jnp.where(group < ys, jnp.where(hit > 0.5, rank, -1.0), weight)
    code = jnp.concatenate([code, jnp.full((lanes - part, lanes), -1.0, jnp.float32)], axis=0)
    table[...] = jnp.transpose(code)[: zs * 2 * ys].reshape(zs, 2 * ys, lanes)
    tables[0] = table[z]
    table_copies = {}
    for d in range(1, zs):
        table_copies[d] = go(
            remote(
                table.at[(z + d) % zs],
                tables.at[PLACE[zs - d]],
                tsend.at[d],
                trecv.at[zs - d],
                at(dz=d),
            )
        )

    best[...] = jnp.full(best.shape, -1e30, jnp.float32)
    total[...] = jnp.zeros(total.shape, jnp.float32)
    accum[...] = jnp.zeros(accum.shape, jnp.float32)

    def attend(pieces, distance=None):
        if distance is not None:
            length = pieces[0][0].shape[0]
            place = lax.broadcasted_iota(jnp.int32, (1, length), 1)
            own_block = (blk - CORES * distance) * count
            other_block = (blk + 1 - 2 * core - CORES * distance) * count
            where = jnp.where(place < count, own_block + place, other_block + place - count)

        def one_head(j, carry):
            parts = [
                lax.dot_general(
                    query[j], keys, (((1,), (1,)), ((), ())), preferred_element_type=jnp.float32
                )
                for keys, unused in pieces
            ]
            if distance is not None:
                valid = where >= begin[:, :1]
                if distance == 0:
                    row = blk * count + lax.broadcasted_iota(jnp.int32, (count, 1), 0)
                    valid = valid & (where <= row)
                parts = [jnp.where(valid, parts[0], -1e30)]
            old = best[j]
            new = old
            for scores in parts:
                new = jnp.maximum(new, jnp.max(scores, axis=1, keepdims=True))
            rescale = jnp.exp(old - new)
            best[j] = new
            summed = total[j] * rescale
            mixed = accum[j] * rescale
            for scores, (unused, values) in zip(parts, pieces):
                weights = jnp.exp(scores - new[:, :1])
                summed = summed + jnp.sum(weights, axis=1, keepdims=True)
                mixed = mixed + jnp.dot(
                    weights.astype(jnp.bfloat16), values, preferred_element_type=jnp.float32
                )
            total[j] = summed
            accum[j] = mixed
            return carry

        lax.fori_loop(0, heads, one_head, 0)

    def attend_fresh(distance):
        for kind in range(2):
            shared[distance, kind].wait_recv()
        attend(
            [
                (
                    fresh[distance, 0].reshape(CORES * count, HD),
                    fresh[distance, 1].reshape(CORES * count, HD),
                )
            ],
            distance,
        )

    def attend_cached(*names):
        pieces = []
        for side, held, batch in names:
            if side == 1:
                onchip[held, batch].wait_recv()
            piece = cached[side, held, batches[batch]]
            piece = piece.reshape(batches[batch].size * prefix_ref.shape[0], 2 * HD)
            pieces.append((piece[:, :HD], piece[:, HD:]))
        attend(pieces)

    ride = {}
    onchip = {}

    def prefix_share(held, batch):
        onchip[held, batch] = go(prefix_core(held, batch))

    def prefix_row(batch):
        for direction in (1, -1):
            ride[(-direction) % ys, batch] = go(prefix_y(0, direction, batch))
        prefix_share(0, batch)

    def prefix_arrived(batch):
        ride[ys - 1, batch].wait_recv()
        if batch == 0:
            ride[2, batch] = go(prefix_y(ys - 1, 1, batch))
        ride[1, batch].wait_recv()
        if batch == 1:
            ride[2, batch] = go(prefix_y(1, -1, batch))
        prefix_share(ys - 1, batch)
        prefix_share(1, batch)

    attend_fresh(0)
    prefix_step(2)
    prefix_row(0)
    fresh_step(1, 0)
    fresh_step(1, 1)
    attend_cached((0, 0, 0), (1, 0, 0))
    prefix_step(3)
    attend_fresh(1)
    fresh_step(2, 0)
    fresh_step(2, 1)
    prefix_step(4)
    prefix_row(1)
    prefix_arrived(0)
    attend_cached((0, ys - 1, 0), (0, 1, 0))
    attend_cached((0, 0, 1), (1, 0, 1))
    fresh_step(3, 0)
    fresh_step(3, 1)
    attend_fresh(2)
    prefix_arrived(1)
    out_ring[3].wait_recv()
    relay_right = go(weights_x(3, 1))
    out_ring[1].wait_recv()
    relay_left = go(weights_x(1, -1))
    out_shared = {held: go(weights_core(held)) for held in (3, 1)}
    attend_cached((1, ys - 1, 0), (1, 1, 0))
    fresh_step(4, 0)
    fresh_step(4, 1)
    attend_cached((0, ys - 1, 1), (0, 1, 1))
    ride[2, 0].wait_recv()
    prefix_share(2, 0)
    attend_cached((1, ys - 1, 1), (1, 1, 1))
    ride[2, 1].wait_recv()
    prefix_share(2, 1)
    attend_fresh(3)
    weight_copies = [
        go(remote(gateup_ref.at[0], gate_up.at[1], ws_send.at[0], ws_recv.at[0], at(other=True))),
        go(remote(down_ref.at[0], down.at[1], ws_send.at[1], ws_recv.at[1], at(other=True))),
    ]
    attend_cached((0, 2, 0), (0, 2, 1))
    attend_fresh(4)
    relay_right.wait_recv()
    relay_left.wait_recv()
    out_shared[2] = go(weights_core(2))
    attend_cached((1, 2, 0), (1, 2, 1))

    for j in range(heads):
        value = (accum[j] / total[j]).astype(jnp.bfloat16)
        context[:, :, j * HD : (j + 1) * HD] = value.reshape(xs, part, HD)
    crossing = {}
    for dx in (2, 1, 3):
        crossing[xs - dx] = go(
            remote(
                context.at[(head + dx) % xs],
                contexts.at[xs - dx],
                cx_send.at[dx],
                cx_recv.at[xs - dx],
                at(dx=dx),
            )
        )
    contexts[0] = context[head]
    out_copy.wait()

    def term(held):
        return jnp.dot(contexts[held], out_weights[held], preferred_element_type=jnp.float32)

    value = hidden_ref[pl.ds(pl.multiple_of(head * part, part), part)].astype(jnp.float32)
    attn = term(0)
    for held in (3, 1, 2):
        out_shared[held].wait_recv()
        crossing[held].wait_recv()
        attn = attn + term(held)
    middle = (value + attn).astype(jnp.bfloat16)
    mid_ref[...] = middle
    wide = middle.astype(jnp.float32)
    scale = lax.rsqrt(jnp.mean(wide * wide, axis=-1, keepdims=True) + 1e-05)
    tokens[0] = (wide * scale * moe_gain_ref[...].reshape(1, width)).astype(jnp.bfloat16)
    half_units = down.shape[1]
    chunk = ROWS_BLOCK // 2

    def token_copy(direction, step, piece):
        held = (-step * direction) % zs
        there = (held - direction) % zs
        number = step * 2 + piece
        side = 0 if direction == 1 else 1
        return pltpu.make_async_remote_copy(
            src_ref=tokens.at[PLACE[held], pl.ds(piece * chunk, chunk)],
            dst_ref=tokens.at[PLACE[there], pl.ds(piece * chunk, chunk)],
            send_sem=zsend.at[side, number],
            recv_sem=zrecv.at[side, number],
            device_id=at(dz=direction),
            device_id_type=MESH,
        )

    reach = zs // 2
    flow = {}
    for direction in (1, -1):
        for step in range(reach):
            for piece in range(2):
                if step < reach - 1 or piece == (0 if direction == 1 else 1):
                    flow[direction, step, piece] = token_copy(direction, step, piece)

    for piece in range(2):
        go(flow[1, 0, piece])
        go(flow[-1, 0, piece])

    slot = lax.broadcasted_iota(jnp.int32, (ys * PIECE, lanes), 0) % PIECE
    slot = slot.astype(jnp.float32)

    def spread(place, first):
        return jnp.concatenate(
            [
                jnp.broadcast_to(tables[place, first + dy : first + dy + 1, :], (PIECE, lanes))
                for dy in range(ys)
            ],
            axis=0,
        )

    def side_of(place):
        return 1 if place % 2 == 0 else -1

    def y_copies(source, target, way, number, send, recv):
        def direct(place, dy):
            return remote(
                source.at[place, dy],
                target.at[place, ys - dy],
                send.at[place, dy],
                recv.at[place, ys - dy],
                at(dy=dy),
            )

        def first_leg(place):
            return remote(
                source.at[place, 2],
                way.at[place],
                vsend.at[number, place],
                vrecv.at[number, place],
                at(dy=side_of(place)),
            )

        def second_leg(place):
            return remote(
                way.at[place],
                target.at[place, 2],
                send.at[place, 2],
                recv.at[place, 2],
                at(dy=side_of(place)),
            )

        def start(place):
            go(first_leg(place))
            go(direct(place, 1))
            go(direct(place, ys - 1))

        def relay(*places):
            for place in places:
                first_leg(place).wait_recv()
                go(second_leg(place))

        def arrived(place):
            direct(place, 1).wait_recv()
            direct(place, ys - 1).wait_recv()
            second_leg(place).wait_recv()

        return start, relay, arrived

    send_pieces, relay_pieces, pieces_here = y_copies(packed, rows, way_out, 0, ysend, yrecv)
    send_backs, relay_backs, backs_here = y_copies(outs, backs, way_back, 1, bsend, brecv)

    def pack(place):
        if place > 0:
            table_copies[(zs - ORDER[place])].wait_recv()
        chosen = jnp.where(spread(place, 0) == slot, 1.0, 0.0).astype(jnp.bfloat16)
        value = jnp.dot(
            chosen[:, :ROWS_BLOCK], tokens[place], preferred_element_type=jnp.float32
        ).astype(jnp.bfloat16)
        value = value.reshape(ys, PIECE, width)
        packed[place, 1:] = value[1:]
        rows[place, 0] = value[0]
        send_pieces(place)

    def experts(first, count):
        for place in range(first, first + count):
            pieces_here(place)
        taken = rows[first : first + count].reshape(count * ys * PIECE, width)
        total = None
        for side in range(2):
            both = jnp.dot(taken, gate_up[side], preferred_element_type=jnp.float32)
            hidden = jax.nn.relu(both[:, :half_units]) * both[:, half_units:]
            term = jnp.dot(
                hidden.astype(jnp.bfloat16), down[side], preferred_element_type=jnp.float32
            )
            total = term if total is None else total + term
        value = total.astype(jnp.bfloat16).reshape(count, ys, PIECE, width)
        outs[first : first + count, 1:] = value[:, 1:]
        backs[first : first + count, 0] = value[:, 0]
        for place in range(first, first + count):
            send_backs(place)

    def combine(place):
        backs_here(place)
        mixing = jnp.where(spread(place, 0) == slot, spread(place, ys), 0.0)
        mixing = mixing.astype(jnp.bfloat16)[:, :ROWS_BLOCK]
        partial[place] = lax.dot_general(
            mixing,
            backs[place].reshape(ys * PIECE, width),
            (((0,), (0,)), ((), ())),
            preferred_element_type=jnp.float32,
        )

    def tokens_step(step):
        for piece in range(2):
            for direction in (1, -1):
                if (direction, step - 1, piece) in flow:
                    flow[direction, step - 1, piece].wait_recv()
                if (direction, step, piece) in flow:
                    go(flow[direction, step, piece])

    pack(0)
    tokens_step(1)
    relay_pieces(0)
    pack(1)
    pack(2)
    for copy in own_copies:
        copy.wait()
    for copy in weight_copies:
        copy.wait_recv()
    tokens_step(2)
    relay_pieces(1, 2)
    pack(3)
    pack(4)
    experts(0, 1)
    tokens_step(3)
    relay_pieces(3, 4)
    pack(5)
    pack(6)
    relay_backs(0)
    experts(1, 2)
    tokens_step(4)
    relay_pieces(5, 6)
    pack(7)
    relay_backs(1, 2)
    experts(3, 2)
    relay_pieces(7)
    combine(0)
    relay_backs(3, 4)
    experts(5, 2)
    combine(1)
    combine(2)
    experts(7, 1)
    relay_backs(5, 6)
    combine(3)
    combine(4)

    def sum_copy(direction, held, piece):
        side = 0 if direction == 1 else 1
        number = (held if direction == 1 else zs - held) * 2 + piece
        source, target = (sums_r, got_r) if direction == 1 else (sums_l, got_l)
        return pltpu.make_async_remote_copy(
            src_ref=source.at[number],
            dst_ref=target.at[number],
            send_sem=ssend.at[side, number],
            recv_sem=srecv.at[side, number],
            device_id=at(dz=direction),
            device_id_type=MESH,
        )

    returned = {}

    def pass_on(direction, distance, piece):
        held = distance if direction == 1 else zs - distance
        number = distance * 2 + piece
        value = partial[PLACE[held], pl.ds(piece * chunk, chunk)]
        source, target = (sums_r, got_r) if direction == 1 else (sums_l, got_l)
        if (direction, distance + 1, piece) in returned:
            returned[direction, distance + 1, piece].wait_recv()
            value = value + target[number + 2].astype(jnp.float32)
        source[number] = value.astype(jnp.bfloat16)
        copy = sum_copy(direction, held, piece)
        returned[direction, distance, piece] = go(copy)

    combine(PLACE[reach - 1])
    pass_on(1, reach - 1, 1)
    combine(PLACE[zs - reach + 1])
    pass_on(-1, reach - 1, 0)
    relay_backs(7)
    combine(PLACE[reach])
    pass_on(1, reach, 0)
    pass_on(-1, reach, 1)
    for distance in range(reach - 1, 0, -1):
        if distance < reach - 1:
            pass_on(1, distance, 1)
            pass_on(-1, distance, 0)
        pass_on(1, distance, 0)
        pass_on(-1, distance, 1)
    for piece in (1, 0):
        spot = pl.ds(piece * chunk, chunk)
        returned[1, 1, piece].wait_recv()
        returned[-1, 1, piece].wait_recv()
        value = (
            mid_ref[spot].astype(jnp.float32)
            + partial[0, spot]
            + got_r[2 + piece].astype(jnp.float32)
            + got_l[2 + piece].astype(jnp.float32)
        ).astype(jnp.bfloat16)
        share = width // xs
        for part_x in range(xs):
            final[part_x, spot] = value[:, part_x * share : (part_x + 1) * share]

    last = []
    for dx in range(1, xs):
        copy = pltpu.make_async_remote_copy(
            src_ref=final.at[(head + dx) % xs],
            dst_ref=landed.at[head],
            send_sem=xsend.at[dx],
            recv_sem=xrecv.at[xs - dx],
            device_id=at(dx=dx),
            device_id_type=MESH,
        )
        go(copy)
        last.append(copy)
    out_ref[head] = final[head]
    for dx in range(1, xs):
        last[xs - dx - 1].wait_recv()
        out_ref[(head + dx) % xs] = landed[(head + dx) % xs]

    for copy in sent:
        copy.wait_send()


def layer(
    sizes,
    hidden,
    gain,
    w_query,
    w_keyval,
    prefix,
    w_out,
    moe_gain,
    w_gateup,
    w_down,
    routes,
    weights,
    lengths,
):
    xs, ys, zs = sizes
    count, width = hidden.shape
    heads = w_query.shape[1] // HD
    part = count // xs
    lanes = 128
    bf16, f32 = jnp.bfloat16, jnp.float32
    half = np.arange(HD // 2, dtype=np.float32)
    freqs = (10000.0 ** (-2.0 * half / HD)).astype(np.float32)
    freqs = jnp.asarray(np.concatenate([freqs, freqs])[None, :])
    dma = pltpu.SemaphoreType.DMA
    vmem = pl.BlockSpec(memory_space=pltpu.VMEM)
    smem = pl.BlockSpec(memory_space=pltpu.SMEM)
    hbm = pl.BlockSpec(memory_space=pl.ANY)
    out = pl.pallas_call(
        functools.partial(layer_kernel, sizes),
        out_shape=jax.ShapeDtypeStruct((xs, part, width // xs), bf16),
        in_specs=[smem, vmem, vmem, vmem, vmem, hbm, vmem, hbm, vmem, vmem, vmem, hbm, hbm],
        out_specs=vmem,
        scratch_shapes=[
            pltpu.VMEM(w_keyval.shape[1:], bf16),
            pltpu.VMEM((CORES, ys, zs, prefix.shape[0], 2 * HD), bf16),
            pltpu.VMEM((PAST + 1, 2, CORES, count, HD), bf16),
            pltpu.VMEM((xs,) + w_out.shape, bf16),
            pltpu.VMEM((heads, count, HD), bf16),
            pltpu.VMEM((count, HD), jnp.int32),
            pltpu.VMEM((heads, count, HD), f32),
            pltpu.VMEM((heads, count, HD), f32),
            pltpu.VMEM((heads, count, HD), f32),
            pltpu.VMEM((xs, part, heads * HD), bf16),
            pltpu.VMEM((xs, part, heads * HD), bf16),
            pltpu.VMEM((part, width), bf16),
            pltpu.VMEM((zs, part, width), bf16),
            pltpu.VMEM((zs, 2 * ys, lanes), f32),
            pltpu.VMEM((zs, 2 * ys, lanes), f32),
            pltpu.VMEM((zs, ys, PIECE, width), bf16),
            pltpu.VMEM((zs, ys, PIECE, width), bf16),
            pltpu.VMEM((zs, ys, PIECE, width), bf16),
            pltpu.VMEM((zs, ys, PIECE, width), bf16),
            pltpu.VMEM((zs, PIECE, width), bf16),
            pltpu.VMEM((zs, PIECE, width), bf16),
            pltpu.VMEM((2,) + w_gateup.shape[1:], bf16),
            pltpu.VMEM((2,) + w_down.shape[1:], bf16),
            pltpu.VMEM((zs, part, width), f32),
            pltpu.VMEM((zs + 2, part // 2, width), bf16),
            pltpu.VMEM((zs + 2, part // 2, width), bf16),
            pltpu.VMEM((zs + 2, part // 2, width), bf16),
            pltpu.VMEM((zs + 2, part // 2, width), bf16),
            pltpu.VMEM((xs, part, width // xs), bf16),
            pltpu.VMEM((xs, part, width // xs), bf16),
            dma((4,)),
            dma((2, zs // 2)),
            dma((2, zs // 2)),
            dma((ys, 2)),
            dma((ys, 2)),
            dma((ys, 2)),
            dma((ys, 2)),
            dma((PAST, 2)),
            dma((PAST, 2)),
            dma((PAST + 1, 2)),
            dma((PAST + 1, 2)),
            dma((xs,)),
            dma((xs,)),
            dma((xs,)),
            dma((xs,)),
            dma((xs,)),
            dma((xs,)),
            dma((2,)),
            dma((2,)),
            dma((zs,)),
            dma((zs,)),
            dma((2, zs)),
            dma((2, zs)),
            dma((zs, ys)),
            dma((zs, ys)),
            dma((zs, ys)),
            dma((zs, ys)),
            dma((2, zs)),
            dma((2, zs)),
            dma((2, zs + 2)),
            dma((2, zs + 2)),
            dma((xs,)),
            dma((xs,)),
        ],
        compiler_params=pltpu.CompilerParams(
            collective_id=0, has_side_effects=True, vmem_limit_bytes=62 * 2**20
        ),
    )(
        lengths,
        hidden,
        gain,
        freqs,
        w_query,
        w_keyval,
        prefix,
        w_out,
        moe_gain,
        routes,
        weights,
        w_gateup,
        w_down,
    )
    return out.reshape(count, width // xs)


def shards(
    hidden_in,
    attn_gain,
    w_query,
    w_keyval,
    prefix_cache,
    w_out,
    moe_gain,
    w_gateup,
    w_down,
    routes,
    route_weights,
    lengths,
):
    chips_z = 8
    sizes = (lax.axis_size("head"), lax.axis_size("blk") // (CORES * chips_z), chips_z)
    return layer(
        sizes,
        hidden_in,
        attn_gain,
        w_query,
        w_keyval,
        prefix_cache,
        w_out,
        moe_gain,
        w_gateup,
        w_down,
        routes,
        route_weights,
        lengths,
    )


def solution(mesh):
    return jax.shard_map(
        shards,
        mesh=mesh,
        in_specs=(
            P("blk", None),
            P(),
            P(None, "head"),
            P(),
            P("blk", None, None),
            P("head", None),
            P(),
            P("blk", None, None),
            P("blk", None, None),
            P("blk", None),
            P("blk", None),
            P(),
        ),
        out_specs=P("blk", "head"),
        check_vma=False,
    )
```

time: 221 us -> 130 us (0.59)
  waiting for transfers between devices: 64.9 us -> 0 us
  Pallas kernels: 72.6 us -> 125 us
  matrix products: 31.1 us -> 0 us
  starting transfers between devices: 17.5 us -> 0 us
  between operations: 14.2 us -> 0.01 us
  other arithmetic: 11.2 us -> 0 us
  local copies, waits for them, and re-layouts: 8.6 us -> 4.56 us
    pallas_call x1, Pallas kernels: 72.6 us -> 125 us  [layer(): pl.pallas_call(functools.partial(layer_kernel, sizes), out_shape=jax.Shap...]
    dot_general x25 -> x0, matrix products: 31.1 us -> none  [the longest x14 15.7 us: matmul(): return jnp.dot(left, right, preferred_element_type=jnp.float32)]
    all_gather x1 -> x0, waiting for transfers between devices: 23.2 us -> none  [shards(): lax.all_gather(cached, 'blk', axis=0, tiled=True)]
    reduce_scatter x1 -> x0, waiting for transfers between devices: 21.7 us -> none  [shards(): lax.psum_scatter(matmul(context, w_out).astype(jnp.bfloat16), 'head', sca...]
    ppermute x8 -> x0, waiting for transfers between devices: 20 us -> none  [passed_along(): return lax.ppermute(value, axis, pairs)]
    ppermute x8 -> x0, starting transfers between devices: 17.5 us -> none  [passed_along(): return lax.ppermute(value, axis, pairs)]
    reduce_sum x8 -> x0, other arithmetic: 8.2 us -> none  [the longest x5 6.61 us: attend(): total = total * rescale + jnp.sum(weights, axis=1)]
    unnamed x62 -> x3, local copies, waits for them, and re-layouts: 4.02 us -> 4.56 us
  transfers between devices with their start and end apart: 10 -> 0, of which waited for: 9 -> 0; matrix products, arithmetic and copies ran while one was open for 10% -> 0% of each run, Pallas kernels for 0% -> 0%
where the time goes in v3:
time: 130 us
  Pallas kernels  125 us (96%)
  local copies, waits for them, and re-layouts  4.56 us (4%)
    pallas_call x1, Pallas kernels, layer(): pl.pallas_call(functools.partial(layer_kernel, sizes), out_shape=jax.Shap...  125 us
    unnamed x3, local copies, waits for them, and re-layouts  4.56 us

profile of v3, /device:TPU:32, one launch (start us, length us, event | category | flops | bytes accessed | tf_op | source)
XLA Modules:
  0.0 129.5 jit_solution(9697647782595987219)
XLA Ops:
  0.0 1.5 %copy.14.routes_ref = s32[256,4]{1,0:T(8,128)} copy(s32[256,4]{0,1:T(4,128)} %param.22) | data formatting | bytes 8192 | tf_op args[9]
  1.5 1.5 %copy.15.weights_ref = f32[256,4]{1,0:T(8,128)} copy(f32[256,4]{0,1:T(4,128)} %param.23) | data formatting | bytes 8192 | tf_op args[10]
  2.9 125.0 %shard_map.127 = bf16[4,64,384]{2,1,0:T(8,128)(2,1)} custom-call(s32[32]{0:T(128)} %lengths_ref.1, bf16[256,1536]{1,0:T(8,128)(2,1)} %hidden_ref.1, f32[1536]{0:T(1024)} %gain_ref.1, f32[1,128]{1,0:T(1,128)} %constant.2.clone.freqs_ref, bf16[1536,384]{1,0:T(8,128)(2,1)} %w_query_ref.1, bf16[2,1536,256]{2,1,0:T(8,128)(2,1)} %w_keyval_ref.1, ...), custom_call_target="tpu_custom_call" | custom-call | tf_op jit(solution)/shard_map/pallas_call | solution.py:787
  127.9 1.6 %copy.17 = bf16[256,384]{1,0:T(8,128)(2,1)} copy(bf16[256,384]{1,0:T(8,128)(2,1)} %bitcast.1) | data formatting | bytes 393216

commit v4 on v3

--- a/solution.py
+++ b/solution.py
@@ -238,7 +238,13 @@
     for r in range(lengths_ref.shape[0]):
         end = end + lengths_ref[r]
         start = jnp.where(token >= end, end, start)
-    begin[...] = start
+    lane_token = blk * count + lax.broadcasted_iota(jnp.int32, (1, count), 1)
+    lane_start = jnp.zeros((1, count), jnp.int32)
+    end = jnp.int32(0)
+    for r in range(lengths_ref.shape[0]):
+        end = end + lengths_ref[r]
+        lane_start = jnp.where(lane_token >= end, end, lane_start)
+    begin[...] = lane_start
     prefix_total = cached.shape[0] * ys * zs * prefix_ref.shape[0]
     angle = (prefix_total + token - start).astype(jnp.float32) * freqs_ref[...]
     cosine = jnp.cos(angle)
@@ -300,31 +306,34 @@
     for j in range(heads):
         query[j] = (turned(queries[:, j * HD : (j + 1) * HD]) * HD ** (-0.5)).astype(jnp.bfloat16)
     lanes = table.shape[2]
-    wanted = routes_ref[pl.ds(pl.multiple_of(head * part, part), part), :]
-    given = weights_ref[pl.ds(pl.multiple_of(head * part, part), part), :]
-    column = lax.broadcasted_iota(jnp.int32, (part, lanes), 1)
-    group = column % (2 * ys)
-    expert = ((y + group % ys) % ys) * zs + column // (2 * ys)
-    hit = jnp.zeros((part, lanes), jnp.float32)
-    weight = jnp.zeros((part, lanes), jnp.float32)
-    for k in range(routes_ref.shape[1]):
-        same = wanted[:, k : k + 1] == expert
+    def quarter_of(ref):
+        return pltpu.roll(ref[...], (xs - head) % xs * part, 1)[:, :lanes]
+
+    row = lax.broadcasted_iota(jnp.int32, (zs * 2 * ys, lanes), 0)
+    wanted = quarter_of(routes_ref)
+    wanted = jnp.where(lax.broadcasted_iota(jnp.int32, wanted.shape, 1) < part, wanted, -1)
+    given = quarter_of(weights_ref)
+    group = row % (2 * ys)
+    expert = ((y + group % ys) % ys) * zs + row // (2 * ys)
+    hit = jnp.zeros((zs * 2 * ys, lanes), jnp.float32)
+    weight = jnp.zeros((zs * 2 * ys, lanes), jnp.float32)
+    for k in range(routes_ref.shape[0]):
+        same = wanted[k : k + 1, :] == expert
         hit = hit + jnp.where(same, 1.0, 0.0)
-        weight = weight + jnp.where(same, given[:, k : k + 1], 0.0)
+        weight = weight + jnp.where(same, given[k : k + 1, :], 0.0)
     before = jnp.where(
-        lax.broadcasted_iota(jnp.int32, (part, part), 1)
-        < lax.broadcasted_iota(jnp.int32, (part, part), 0),
+        lax.broadcasted_iota(jnp.int32, (lanes, lanes), 0)
+        < lax.broadcasted_iota(jnp.int32, (lanes, lanes), 1),
         1.0,
         0.0,
     )
     rank = jnp.dot(
+        hit.astype(jnp.bfloat16),
         before.astype(jnp.bfloat16),
-        hit.astype(jnp.bfloat16),
         preferred_element_type=jnp.float32,
     )
     code = jnp.where(group < ys, jnp.where(hit > 0.5, rank, -1.0), weight)
-    code = jnp.concatenate([code, jnp.full((lanes - part, lanes), -1.0, jnp.float32)], axis=0)
-    table[...] = jnp.transpose(code)[: zs * 2 * ys].reshape(zs, 2 * ys, lanes)
+    table[...] = code.reshape(zs, 2 * ys, lanes)
     tables[0] = table[z]
     table_copies = {}
     for d in range(1, zs):
@@ -342,43 +351,33 @@
     total[...] = jnp.zeros(total.shape, jnp.float32)
     accum[...] = jnp.zeros(accum.shape, jnp.float32)
 
-    def attend(pieces, distance=None):
+    def attend(keys, values, distance=None):
+        length = keys.shape[0]
+        turned_values = jnp.transpose(values)
         if distance is not None:
-            length = pieces[0][0].shape[0]
-            place = lax.broadcasted_iota(jnp.int32, (1, length), 1)
+            place = lax.broadcasted_iota(jnp.int32, (length, 1), 0)
             own_block = (blk - CORES * distance) * count
             other_block = (blk + 1 - 2 * core - CORES * distance) * count
             where = jnp.where(place < count, own_block + place, other_block + place - count)
 
         def one_head(j, carry):
-            parts = [
-                lax.dot_general(
-                    query[j], keys, (((1,), (1,)), ((), ())), preferred_element_type=jnp.float32
-                )
-                for keys, unused in pieces
-            ]
+            scores = lax.dot_general(
+                keys, query[j], (((1,), (1,)), ((), ())), preferred_element_type=jnp.float32
+            )
             if distance is not None:
-                valid = where >= begin[:, :1]
+                valid = where >= begin[...]
                 if distance == 0:
-                    row = blk * count + lax.broadcasted_iota(jnp.int32, (count, 1), 0)
-                    valid = valid & (where <= row)
-                parts = [jnp.where(valid, parts[0], -1e30)]
+                    valid = valid & (where <= lane_token)
+                scores = jnp.where(valid, scores, -1e30)
             old = best[j]
-            new = old
-            for scores in parts:
-                new = jnp.maximum(new, jnp.max(scores, axis=1, keepdims=True))
+            new = jnp.maximum(old, jnp.max(scores, axis=0, keepdims=True))
+            weights = jnp.exp(scores - new)
             rescale = jnp.exp(old - new)
             best[j] = new
-            summed = total[j] * rescale
-            mixed = accum[j] * rescale
-            for scores, (unused, values) in zip(parts, pieces):
-                weights = jnp.exp(scores - new[:, :1])
-                summed = summed + jnp.sum(weights, axis=1, keepdims=True)
-                mixed = mixed + jnp.dot(
-                    weights.astype(jnp.bfloat16), values, preferred_element_type=jnp.float32
-                )
-            total[j] = summed
-            accum[j] = mixed
+            total[j] = total[j] * rescale + jnp.sum(weights, axis=0, keepdims=True)
+            accum[j] = accum[j] * rescale + jnp.dot(
+                turned_values, weights.astype(jnp.bfloat16), preferred_element_type=jnp.float32
+            )
             return carry
 
         lax.fori_loop(0, heads, one_head, 0)
@@ -387,12 +386,8 @@
         for kind in range(2):
             shared[distance, kind].wait_recv()
         attend(
-            [
-                (
-                    fresh[distance, 0].reshape(CORES * count, HD),
-                    fresh[distance, 1].reshape(CORES * count, HD),
-                )
-            ],
+            fresh[distance, 0].reshape(CORES * count, HD),
+            fresh[distance, 1].reshape(CORES * count, HD),
             distance,
         )
 
@@ -403,8 +398,9 @@
                 onchip[held, batch].wait_recv()
             piece = cached[side, held, batches[batch]]
             piece = piece.reshape(batches[batch].size * prefix_ref.shape[0], 2 * HD)
-            pieces.append((piece[:, :HD], piece[:, HD:]))
-        attend(pieces)
+            pieces.append(piece)
+        whole = jnp.concatenate(pieces, axis=0)
+        attend(whole[:, :HD], whole[:, HD:])
 
     ride = {}
     onchip = {}
@@ -473,7 +469,7 @@
     attend_cached((1, 2, 0), (1, 2, 1))
 
     for j in range(heads):
-        value = (accum[j] / total[j]).astype(jnp.bfloat16)
+        value = jnp.transpose(accum[j] / total[j]).astype(jnp.bfloat16)
         context[:, :, j * HD : (j + 1) * HD] = value.reshape(xs, part, HD)
     crossing = {}
     for dx in (2, 1, 3):
@@ -576,7 +572,7 @@
             )
 
         def start(place):
-            go(first_leg(place))
+            go(direct(place, 2) if place == zs - 1 else first_leg(place))
             go(direct(place, 1))
             go(direct(place, ys - 1))
 
@@ -588,7 +584,7 @@
         def arrived(place):
             direct(place, 1).wait_recv()
             direct(place, ys - 1).wait_recv()
-            second_leg(place).wait_recv()
+            (direct if place == zs - 1 else lambda at_place, dy: second_leg(at_place))(place, 2).wait_recv()
 
         return start, relay, arrived
 
@@ -657,25 +653,21 @@
     relay_pieces(1, 2)
     pack(3)
     pack(4)
-    experts(0, 1)
     tokens_step(3)
     relay_pieces(3, 4)
     pack(5)
     pack(6)
-    relay_backs(0)
-    experts(1, 2)
+    experts(0, 3)
     tokens_step(4)
     relay_pieces(5, 6)
     pack(7)
-    relay_backs(1, 2)
+    relay_backs(0, 1, 2)
     experts(3, 2)
-    relay_pieces(7)
     combine(0)
-    relay_backs(3, 4)
-    experts(5, 2)
     combine(1)
     combine(2)
-    experts(7, 1)
+    relay_backs(3, 4)
+    experts(5, 3)
     relay_backs(5, 6)
     combine(3)
     combine(4)
@@ -711,7 +703,6 @@
     pass_on(1, reach - 1, 1)
     combine(PLACE[zs - reach + 1])
     pass_on(-1, reach - 1, 0)
-    relay_backs(7)
     combine(PLACE[reach])
     pass_on(1, reach, 0)
     pass_on(-1, reach, 1)
@@ -795,10 +786,10 @@
             pltpu.VMEM((PAST + 1, 2, CORES, count, HD), bf16),
             pltpu.VMEM((xs,) + w_out.shape, bf16),
             pltpu.VMEM((heads, count, HD), bf16),
-            pltpu.VMEM((count, HD), jnp.int32),
-            pltpu.VMEM((heads, count, HD), f32),
-            pltpu.VMEM((heads, count, HD), f32),
-            pltpu.VMEM((heads, count, HD), f32),
+            pltpu.VMEM((1, count), jnp.int32),
+            pltpu.VMEM((heads, 1, count), f32),
+            pltpu.VMEM((heads, 1, count), f32),
+            pltpu.VMEM((heads, HD, count), f32),
             pltpu.VMEM((xs, part, heads * HD), bf16),
             pltpu.VMEM((xs, part, heads * HD), bf16),
             pltpu.VMEM((part, width), bf16),
@@ -867,8 +858,8 @@
         prefix,
         w_out,
         moe_gain,
-        routes,
-        weights,
+        routes.T,
+        weights.T,
         w_gateup,
         w_down,
     )

time: 130 us -> 125 us (0.962)
  local copies, waits for them, and re-layouts: 4.56 us -> 1.62 us
  Pallas kernels: 125 us -> 123 us
    unnamed x3 -> x1, local copies, waits for them, and re-layouts: 4.56 us -> 1.62 us
    pallas_call x1, Pallas kernels: 125 us -> 123 us  [layer(): pl.pallas_call(functools.partial(layer_kernel, sizes), out_shape=jax.Shap...]
where the time goes in v4:
time: 125 us; the launch traced here: 124 us
  Pallas kernels  123 us (98%)
  local copies, waits for them, and re-layouts  1.62 us (1%)
    pallas_call x1, Pallas kernels, layer(): pl.pallas_call(functools.partial(layer_kernel, sizes), out_shape=jax.Shap...  123 us

profile of v4, /device:TPU:32, one launch (start us, length us, event | category | flops | bytes accessed | tf_op | source)
XLA Modules:
  0.0 124.3 jit_solution(5157914048084734561)
XLA Ops:
  0.0 122.7 %shard_map.127 = bf16[4,64,384]{2,1,0:T(8,128)(2,1)} custom-call(s32[32]{0:T(128)} %lengths_ref.1, bf16[256,1536]{1,0:T(8,128)(2,1)} %hidden_ref.1, f32[1536]{0:T(1024)} %gain_ref.1, f32[1,128]{1,0:T(1,128)} %constant.2.clone.freqs_ref, bf16[1536,384]{1,0:T(8,128)(2,1)} %w_query_ref.1, bf16[2,1536,256]{2,1,0:T(8,128)(2,1)} %w_keyval_ref.1, ...), custom_call_target="tpu_custom_call" | custom-call | tf_op jit(solution)/shard_map/pallas_call | solution.py:778
  122.7 1.6 %copy.15 = bf16[256,384]{1,0:T(8,128)(2,1)} copy(bf16[256,384]{1,0:T(8,128)(2,1)} %bitcast.3) | data formatting | bytes 393216

commit v5 on v4

--- a/solution.py
+++ b/solution.py
@@ -59,10 +59,8 @@
     gate_up,
     down,
     partial,
-    sums_r,
-    sums_l,
-    got_r,
-    got_l,
+    sums,
+    got,
     final,
     landed,
     local_sem,
@@ -500,6 +498,7 @@
     scale = lax.rsqrt(jnp.mean(wide * wide, axis=-1, keepdims=True) + 1e-05)
     tokens[0] = (wide * scale * moe_gain_ref[...].reshape(1, width)).astype(jnp.bfloat16)
     half_units = down.shape[1]
+    split = width // 2
     chunk = ROWS_BLOCK // 2
 
     def token_copy(direction, step, piece):
@@ -541,7 +540,7 @@
         )
 
     def side_of(place):
-        return 1 if place % 2 == 0 else -1
+        return 1 if (place + place // zs) % 2 == 0 else -1
 
     def y_copies(source, target, way, number, send, recv):
         def direct(place, dy):
@@ -572,7 +571,7 @@
             )
 
         def start(place):
-            go(direct(place, 2) if place == zs - 1 else first_leg(place))
+            go(direct(place, 2) if place % zs == zs - 1 else first_leg(place))
             go(direct(place, 1))
             go(direct(place, ys - 1))
 
@@ -584,7 +583,7 @@
         def arrived(place):
             direct(place, 1).wait_recv()
             direct(place, ys - 1).wait_recv()
-            (direct if place == zs - 1 else lambda at_place, dy: second_leg(at_place))(place, 2).wait_recv()
+            (direct(place, 2) if place % zs == zs - 1 else second_leg(place)).wait_recv()
 
         return start, relay, arrived
 
@@ -607,27 +606,32 @@
         for place in range(first, first + count):
             pieces_here(place)
         taken = rows[first : first + count].reshape(count * ys * PIECE, width)
-        total = None
+        hidden = []
         for side in range(2):
             both = jnp.dot(taken, gate_up[side], preferred_element_type=jnp.float32)
-            hidden = jax.nn.relu(both[:, :half_units]) * both[:, half_units:]
-            term = jnp.dot(
-                hidden.astype(jnp.bfloat16), down[side], preferred_element_type=jnp.float32
+            both = jax.nn.relu(both[:, :half_units]) * both[:, half_units:]
+            hidden.append(both.astype(jnp.bfloat16))
+        for columns in range(2):
+            span = slice(columns * split, (columns + 1) * split)
+            value = jnp.dot(hidden[0], down[0, :, span], preferred_element_type=jnp.float32)
+            value = value + jnp.dot(
+                hidden[1], down[1, :, span], preferred_element_type=jnp.float32
             )
-            total = term if total is None else total + term
-        value = total.astype(jnp.bfloat16).reshape(count, ys, PIECE, width)
-        outs[first : first + count, 1:] = value[:, 1:]
-        backs[first : first + count, 0] = value[:, 0]
-        for place in range(first, first + count):
+            value = value.astype(jnp.bfloat16).reshape(count, ys, PIECE, split)
+            base = columns * zs + first
+            outs[base : base + count, 1:] = value[:, 1:]
+            backs[base : base + count, 0] = value[:, 0]
+        for place in reversed(range(first, first + count)):
             send_backs(place)
 
     def combine(place):
         backs_here(place)
-        mixing = jnp.where(spread(place, 0) == slot, spread(place, ys), 0.0)
-        mixing = mixing.astype(jnp.bfloat16)[:, :ROWS_BLOCK]
+        mixing = jnp.where(
+            spread(place % zs, 0) == slot, spread(place % zs, ys), 0.0
+        ).astype(jnp.bfloat16)[:, :ROWS_BLOCK]
         partial[place] = lax.dot_general(
             mixing,
-            backs[place].reshape(ys * PIECE, width),
+            backs[place].reshape(ys * PIECE, split),
             (((0,), (0,)), ((), ())),
             preferred_element_type=jnp.float32,
         )
@@ -668,63 +672,85 @@
     combine(2)
     relay_backs(3, 4)
     experts(5, 3)
-    relay_backs(5, 6)
+    for place in reversed(range(zs)):
+        send_backs(zs + place)
     combine(3)
     combine(4)
-
-    def sum_copy(direction, held, piece):
-        side = 0 if direction == 1 else 1
-        number = (held if direction == 1 else zs - held) * 2 + piece
-        source, target = (sums_r, got_r) if direction == 1 else (sums_l, got_l)
-        return pltpu.make_async_remote_copy(
-            src_ref=source.at[number],
-            dst_ref=target.at[number],
-            send_sem=ssend.at[side, number],
-            recv_sem=srecv.at[side, number],
-            device_id=at(dz=direction),
-            device_id_type=MESH,
-        )
+    relay_backs(6, 5)
 
     returned = {}
 
-    def pass_on(direction, distance, piece):
+    def pass_on(columns, direction, distance, piece):
         held = distance if direction == 1 else zs - distance
         number = distance * 2 + piece
-        value = partial[PLACE[held], pl.ds(piece * chunk, chunk)]
-        source, target = (sums_r, got_r) if direction == 1 else (sums_l, got_l)
-        if (direction, distance + 1, piece) in returned:
-            returned[direction, distance + 1, piece].wait_recv()
-            value = value + target[number + 2].astype(jnp.float32)
-        source[number] = value.astype(jnp.bfloat16)
-        copy = sum_copy(direction, held, piece)
-        returned[direction, distance, piece] = go(copy)
-
-    combine(PLACE[reach - 1])
-    pass_on(1, reach - 1, 1)
-    combine(PLACE[zs - reach + 1])
-    pass_on(-1, reach - 1, 0)
-    combine(PLACE[reach])
-    pass_on(1, reach, 0)
-    pass_on(-1, reach, 1)
-    for distance in range(reach - 1, 0, -1):
+        side = columns * 2 + (0 if direction == 1 else 1)
+        value = partial[columns * zs + PLACE[held], pl.ds(piece * chunk, chunk)]
+        before_it = returned.get((columns, direction, distance + 1, piece))
+        if before_it is not None:
+            before_it.wait_recv()
+            value = value + got[side, number + 2].astype(jnp.float32)
+        sums[side, number] = value.astype(jnp.bfloat16)
+        returned[columns, direction, distance, piece] = go(
+            remote(
+                sums.at[side, number],
+                got.at[side, number],
+                ssend.at[side, number],
+                srecv.at[side, number],
+                at(dz=direction),
+            )
+        )
+
+    def far_sums(columns):
+        combine(columns * zs + PLACE[reach])
+        pass_on(columns, 1, reach, 0)
+        pass_on(columns, -1, reach, 1)
+        combine(columns * zs + PLACE[reach - 1])
+        pass_on(columns, 1, reach - 1, 1)
+        combine(columns * zs + PLACE[zs - reach + 1])
+        pass_on(columns, -1, reach - 1, 0)
+
+    def near_sums(columns, distance):
         if distance < reach - 1:
-            pass_on(1, distance, 1)
-            pass_on(-1, distance, 0)
-        pass_on(1, distance, 0)
-        pass_on(-1, distance, 1)
-    for piece in (1, 0):
-        spot = pl.ds(piece * chunk, chunk)
-        returned[1, 1, piece].wait_recv()
-        returned[-1, 1, piece].wait_recv()
-        value = (
-            mid_ref[spot].astype(jnp.float32)
-            + partial[0, spot]
-            + got_r[2 + piece].astype(jnp.float32)
-            + got_l[2 + piece].astype(jnp.float32)
-        ).astype(jnp.bfloat16)
+            pass_on(columns, 1, distance, 1)
+            pass_on(columns, -1, distance, 0)
+        pass_on(columns, 1, distance, 0)
+        pass_on(columns, -1, distance, 1)
+
+    def finish(columns):
         share = width // xs
-        for part_x in range(xs):
-            final[part_x, spot] = value[:, part_x * share : (part_x + 1) * share]
+        for piece in (1, 0):
+            spot = pl.ds(piece * chunk, chunk)
+            for direction in (1, -1):
+                returned[columns, direction, 1, piece].wait_recv()
+            value = (
+                mid_ref[spot, columns * split : (columns + 1) * split].astype(jnp.float32)
+                + partial[columns * zs, spot]
+                + got[columns * 2, 2 + piece].astype(jnp.float32)
+                + got[columns * 2 + 1, 2 + piece].astype(jnp.float32)
+            ).astype(jnp.bfloat16)
+            for number in range(split // share):
+                final[columns * (split // share) + number, spot] = value[
+                    :, number * share : (number + 1) * share
+                ]
+
+    far_sums(0)
+    relay_backs(zs + 6, zs + 5)
+    near_sums(0, 3)
+    relay_backs(zs + 4, zs + 3)
+    near_sums(0, 2)
+    relay_backs(zs + 2, zs + 1, zs)
+    far_sums(1)
+    near_sums(0, 1)
+    combine(zs + 4)
+    combine(zs + 3)
+    near_sums(1, 3)
+    combine(zs + 2)
+    combine(zs + 1)
+    combine(zs)
+    finish(0)
+    near_sums(1, 2)
+    near_sums(1, 1)
+    finish(1)
 
     last = []
     for dx in range(1, xs):
@@ -798,17 +824,15 @@
             pltpu.VMEM((zs, 2 * ys, lanes), f32),
             pltpu.VMEM((zs, ys, PIECE, width), bf16),
             pltpu.VMEM((zs, ys, PIECE, width), bf16),
-            pltpu.VMEM((zs, ys, PIECE, width), bf16),
-            pltpu.VMEM((zs, ys, PIECE, width), bf16),
+            pltpu.VMEM((2 * zs, ys, PIECE, width // 2), bf16),
+            pltpu.VMEM((2 * zs, ys, PIECE, width // 2), bf16),
             pltpu.VMEM((zs, PIECE, width), bf16),
-            pltpu.VMEM((zs, PIECE, width), bf16),
+            pltpu.VMEM((2 * zs, PIECE, width // 2), bf16),
             pltpu.VMEM((2,) + w_gateup.shape[1:], bf16),
             pltpu.VMEM((2,) + w_down.shape[1:], bf16),
-            pltpu.VMEM((zs, part, width), f32),
-            pltpu.VMEM((zs + 2, part // 2, width), bf16),
-            pltpu.VMEM((zs + 2, part // 2, width), bf16),
-            pltpu.VMEM((zs + 2, part // 2, width), bf16),
-            pltpu.VMEM((zs + 2, part // 2, width), bf16),
+            pltpu.VMEM((2 * zs, part, width // 2), f32),
+            pltpu.VMEM((4, zs + 2, part // 2, width // 2), bf16),
+            pltpu.VMEM((4, zs + 2, part // 2, width // 2), bf16),
             pltpu.VMEM((xs, part, width // xs), bf16),
             pltpu.VMEM((xs, part, width // xs), bf16),
             dma((4,)),
@@ -836,12 +860,12 @@
             dma((2, zs)),
             dma((zs, ys)),
             dma((zs, ys)),
-            dma((zs, ys)),
-            dma((zs, ys)),
-            dma((2, zs)),
-            dma((2, zs)),
-            dma((2, zs + 2)),
-            dma((2, zs + 2)),
+            dma((2 * zs, ys)),
+            dma((2 * zs, ys)),
+            dma((2, 2 * zs)),
+            dma((2, 2 * zs)),
+            dma((4, zs + 2)),
+            dma((4, zs + 2)),
             dma((xs,)),
             dma((xs,)),
         ],

time: 125 us -> 125 us (level)
  no operation moved by 1% of the time
where the time goes in v5:
time: 125 us; the launch traced here: 124 us
  Pallas kernels  122 us (98%)
  local copies, waits for them, and re-layouts  1.62 us (1%)
    pallas_call x1, Pallas kernels, layer(): pl.pallas_call(functools.partial(layer_kernel, sizes), out_shape=jax.Shap...  122 us

profile of v5, /device:TPU:32, one launch (start us, length us, event | category | flops | bytes accessed | tf_op | source)
XLA Modules:
  0.0 123.9 jit_solution(908890315964609612)
XLA Ops:
  0.0 122.3 %shard_map.127 = bf16[4,64,384]{2,1,0:T(8,128)(2,1)} custom-call(s32[32]{0:T(128)} %lengths_ref.1, bf16[256,1536]{1,0:T(8,128)(2,1)} %hidden_ref.1, f32[1536]{0:T(1024)} %gain_ref.1, f32[1,128]{1,0:T(1,128)} %constant.2.clone.freqs_ref, bf16[1536,384]{1,0:T(8,128)(2,1)} %w_query_ref.1, bf16[2,1536,256]{2,1,0:T(8,128)(2,1)} %w_keyval_ref.1, ...), custom_call_target="tpu_custom_call" | custom-call | tf_op jit(solution)/shard_map/pallas_call | solution.py:804
  122.3 1.6 %copy.15 = bf16[256,384]{1,0:T(8,128)(2,1)} copy(bf16[256,384]{1,0:T(8,128)(2,1)} %bitcast.3) | data formatting | bytes 393216

commit v6 on v5

--- a/solution.py
+++ b/solution.py
@@ -45,7 +45,8 @@
     total,
     accum,
     context,
-    contexts,
+    terms,
+    terms_in,
     mid_ref,
     tokens,
     table,
@@ -74,10 +75,6 @@
     nz_recv,
     nc_send,
     nc_recv,
-    wx_send,
-    wx_recv,
-    wc_send,
-    wc_recv,
     cx_send,
     cx_recv,
     ws_send,
@@ -107,7 +104,6 @@
     count, width = hidden_ref.shape
     heads = query.shape[0]
     part = count // xs
-    half = w_out_ref.shape[0] // CORES
 
     def at(dx=0, dy=0, dz=0, other=False):
         cc = 1 - core if other else core
@@ -142,7 +138,7 @@
 
     kv_copy = pltpu.make_async_copy(w_keyval_ref.at[head // (xs // KVH)], w_kv, local_sem.at[0])
     kv_copy.start()
-    out_copy = pltpu.make_async_copy(w_out_ref, out_weights.at[0], local_sem.at[1])
+    out_copy = pltpu.make_async_copy(w_out_ref, out_weights, local_sem.at[1])
     out_copy.start()
     own_copies = [
         pltpu.make_async_copy(gateup_ref.at[0], gate_up.at[0], local_sem.at[2]),
@@ -200,35 +196,6 @@
     flow = {}
     flow[1, 0] = go(prefix_z(1, 0))
     flow[-1, 0] = go(prefix_z(-1, 0))
-
-    mine = pl.ds(pl.multiple_of(core * half, 64), half)
-
-    def weights_x(held, direction):
-        there = (held - direction) % xs
-        rows = mine
-        if held != 0:
-            offset = 0 if direction == 1 else half // 2
-            rows = pl.ds(pl.multiple_of(core * half + offset, 32), half // 2)
-        number = there if held == 0 else (0 if direction == 1 else 2)
-        source = w_out_ref.at[rows] if held == 0 else out_weights.at[held, rows]
-        return remote(
-            source,
-            out_weights.at[there, rows],
-            wx_send.at[number],
-            wx_recv.at[number],
-            at(dx=direction),
-        )
-
-    def weights_core(held):
-        return remote(
-            out_weights.at[held, mine],
-            out_weights.at[held, mine],
-            wc_send.at[held],
-            wc_recv.at[held],
-            at(other=True),
-        )
-
-    out_ring = {3: go(weights_x(0, 1)), 1: go(weights_x(0, -1))}
 
     token = blk * count + lax.broadcasted_iota(jnp.int32, (count, HD), 0)
     start = jnp.zeros((count, HD), jnp.int32)
@@ -440,11 +407,6 @@
     fresh_step(3, 1)
     attend_fresh(2)
     prefix_arrived(1)
-    out_ring[3].wait_recv()
-    relay_right = go(weights_x(3, 1))
-    out_ring[1].wait_recv()
-    relay_left = go(weights_x(1, -1))
-    out_shared = {held: go(weights_core(held)) for held in (3, 1)}
     attend_cached((1, ys - 1, 0), (1, 1, 0))
     fresh_step(4, 0)
     fresh_step(4, 1)
@@ -461,37 +423,54 @@
     ]
     attend_cached((0, 2, 0), (0, 2, 1))
     attend_fresh(4)
-    relay_right.wait_recv()
-    relay_left.wait_recv()
-    out_shared[2] = go(weights_core(2))
     attend_cached((1, 2, 0), (1, 2, 1))
 
     for j in range(heads):
         value = jnp.transpose(accum[j] / total[j]).astype(jnp.bfloat16)
         context[:, :, j * HD : (j + 1) * HD] = value.reshape(xs, part, HD)
-    crossing = {}
-    for dx in (2, 1, 3):
-        crossing[xs - dx] = go(
+    out_copy.wait()
+    piece_rows = part // 2
+
+    def term(dx):
+        return jnp.dot(
+            context[(head + dx) % xs], out_weights[...], preferred_element_type=jnp.float32
+        )
+
+    def send_terms(number, value, dx):
+        terms[number] = value.astype(jnp.bfloat16)
+        return go(
             remote(
-                context.at[(head + dx) % xs],
-                contexts.at[xs - dx],
-                cx_send.at[dx],
-                cx_recv.at[xs - dx],
+                terms.at[number],
+                terms_in.at[number],
+                cx_send.at[number],
+                cx_recv.at[number],
                 at(dx=dx),
             )
         )
-    contexts[0] = context[head]
-    out_copy.wait()
-
-    def term(held):
-        return jnp.dot(contexts[held], out_weights[held], preferred_element_type=jnp.float32)
-
+
+    value = term(2)
+    crossing = [send_terms(0, value[:piece_rows], 1), send_terms(1, value[piece_rows:], -1)]
+    right = term(1)
+    crossing.append(send_terms(2, right[piece_rows:], 1))
+    left = term(-1)
+    crossing.append(send_terms(3, left[:piece_rows], -1))
+    crossing[0].wait_recv()
+    value = right[:piece_rows] + terms_in[0].astype(jnp.float32)
+    crossing.append(send_terms(4, value, 1))
+    crossing[1].wait_recv()
+    value = left[piece_rows:] + terms_in[1].astype(jnp.float32)
+    crossing.append(send_terms(5, value, -1))
     value = hidden_ref[pl.ds(pl.multiple_of(head * part, part), part)].astype(jnp.float32)
-    attn = term(0)
-    for held in (3, 1, 2):
-        out_shared[held].wait_recv()
-        crossing[held].wait_recv()
-        attn = attn + term(held)
+    value = value + term(0)
+    for number in range(2, 6):
+        crossing[number].wait_recv()
+    attn = jnp.concatenate(
+        [
+            terms_in[3].astype(jnp.float32) + terms_in[4].astype(jnp.float32),
+            terms_in[2].astype(jnp.float32) + terms_in[5].astype(jnp.float32),
+        ],
+        axis=0,
+    )
     middle = (value + attn).astype(jnp.bfloat16)
     mid_ref[...] = middle
     wide = middle.astype(jnp.float32)
@@ -810,14 +789,15 @@
             pltpu.VMEM(w_keyval.shape[1:], bf16),
             pltpu.VMEM((CORES, ys, zs, prefix.shape[0], 2 * HD), bf16),
             pltpu.VMEM((PAST + 1, 2, CORES, count, HD), bf16),
-            pltpu.VMEM((xs,) + w_out.shape, bf16),
+            pltpu.VMEM(w_out.shape, bf16),
             pltpu.VMEM((heads, count, HD), bf16),
             pltpu.VMEM((1, count), jnp.int32),
             pltpu.VMEM((heads, 1, count), f32),
             pltpu.VMEM((heads, 1, count), f32),
             pltpu.VMEM((heads, HD, count), f32),
             pltpu.VMEM((xs, part, heads * HD), bf16),
-            pltpu.VMEM((xs, part, heads * HD), bf16),
+            pltpu.VMEM((6, part // 2, width), bf16),
+            pltpu.VMEM((6, part // 2, width), bf16),
             pltpu.VMEM((part, width), bf16),
             pltpu.VMEM((zs, part, width), bf16),
             pltpu.VMEM((zs, 2 * ys, lanes), f32),
@@ -846,12 +826,8 @@
             dma((PAST, 2)),
             dma((PAST + 1, 2)),
             dma((PAST + 1, 2)),
-            dma((xs,)),
-            dma((xs,)),
-            dma((xs,)),
-            dma((xs,)),
-            dma((xs,)),
-            dma((xs,)),
+            dma((6,)),
+            dma((6,)),
             dma((2,)),
             dma((2,)),
             dma((zs,)),

time: 125 us -> 128 us (1.024)
  Pallas kernels: 122 us -> 126 us
    pallas_call x1, Pallas kernels: 122 us -> 126 us  [layer(): pl.pallas_call(functools.partial(layer_kernel, sizes), out_shape=jax.Shap...]
where the time goes in v6:
time: 128 us; the launch traced here: 127 us
  Pallas kernels  126 us (98%)
  local copies, waits for them, and re-layouts  1.62 us (1%)
    pallas_call x1, Pallas kernels, layer(): pl.pallas_call(functools.partial(layer_kernel, sizes), out_shape=jax.Shap...  126 us

profile of v6, /device:TPU:32, one launch (start us, length us, event | category | flops | bytes accessed | tf_op | source)
XLA Modules:
  0.0 127.3 jit_solution(762789283109362210)
XLA Ops:
  0.0 125.7 %shard_map.127 = bf16[4,64,384]{2,1,0:T(8,128)(2,1)} custom-call(s32[32]{0:T(128)} %lengths_ref.1, bf16[256,1536]{1,0:T(8,128)(2,1)} %hidden_ref.1, f32[1536]{0:T(1024)} %gain_ref.1, f32[1,128]{1,0:T(1,128)} %constant.2.clone.freqs_ref, bf16[1536,384]{1,0:T(8,128)(2,1)} %w_query_ref.1, bf16[2,1536,256]{2,1,0:T(8,128)(2,1)} %w_keyval_ref.1, ...), custom_call_target="tpu_custom_call" | custom-call | tf_op jit(solution)/shard_map/pallas_call | solution.py:783
  125.7 1.6 %copy.15 = bf16[256,384]{1,0:T(8,128)(2,1)} copy(bf16[256,384]{1,0:T(8,128)(2,1)} %bitcast.3) | data formatting | bytes 393216

commit v7 on v5

--- a/solution.py
+++ b/solution.py
@@ -62,7 +62,6 @@
     sums,
     got,
     final,
-    landed,
     local_sem,
     pz_send,
     pz_recv,
@@ -716,6 +715,16 @@
         pass_on(columns, 1, distance, 0)
         pass_on(columns, -1, distance, 1)
 
+    def last_copy(dx, piece):
+        spot = pl.ds(piece * chunk, chunk)
+        return remote(
+            final.at[(head + dx) % xs, spot],
+            out_ref.at[head, spot],
+            xsend.at[dx, piece],
+            xrecv.at[xs - dx, piece],
+            at(dx=dx),
+        )
+
     def finish(columns):
         share = width // xs
         for piece in (1, 0):
@@ -732,6 +741,12 @@
                 final[columns * (split // share) + number, spot] = value[
                     :, number * share : (number + 1) * share
                 ]
+            for dx in range(1, xs):
+
+                @pl.when((head + dx) % xs // (split // share) == columns)
+                def _():
+                    last_copy(dx, piece).start()
+
 
     far_sums(0)
     relay_backs(zs + 6, zs + 5)
@@ -752,22 +767,10 @@
     near_sums(1, 1)
     finish(1)
 
-    last = []
-    for dx in range(1, xs):
-        copy = pltpu.make_async_remote_copy(
-            src_ref=final.at[(head + dx) % xs],
-            dst_ref=landed.at[head],
-            send_sem=xsend.at[dx],
-            recv_sem=xrecv.at[xs - dx],
-            device_id=at(dx=dx),
-            device_id_type=MESH,
-        )
-        go(copy)
-        last.append(copy)
     out_ref[head] = final[head]
-    for dx in range(1, xs):
-        last[xs - dx - 1].wait_recv()
-        out_ref[(head + dx) % xs] = landed[(head + dx) % xs]
+    for piece in (1, 0):
+        for dx in range(1, xs):
+            last_copy(dx, piece).wait()
 
     for copy in sent:
         copy.wait_send()
@@ -834,7 +837,6 @@
             pltpu.VMEM((4, zs + 2, part // 2, width // 2), bf16),
             pltpu.VMEM((4, zs + 2, part // 2, width // 2), bf16),
             pltpu.VMEM((xs, part, width // xs), bf16),
-            pltpu.VMEM((xs, part, width // xs), bf16),
             dma((4,)),
             dma((2, zs // 2)),
             dma((2, zs // 2)),
@@ -866,8 +868,8 @@
             dma((2, 2 * zs)),
             dma((4, zs + 2)),
             dma((4, zs + 2)),
-            dma((xs,)),
-            dma((xs,)),
+            dma((xs, 2)),
+            dma((xs, 2)),
         ],
         compiler_params=pltpu.CompilerParams(
             collective_id=0, has_side_effects=True, vmem_limit_bytes=62 * 2**20

time: 125 us -> 124 us (level); the launches traced: 124 us -> 121 us
  Pallas kernels: 122 us -> 120 us
    pallas_call x1, Pallas kernels: 122 us -> 120 us  [layer(): pl.pallas_call(functools.partial(layer_kernel, sizes), out_shape=jax.Shap...]
where the time goes in v7:
time: 124 us; the launch traced here: 121 us
  Pallas kernels  120 us (97%)
  local copies, waits for them, and re-layouts  1.62 us (1%)
    pallas_call x1, Pallas kernels, layer(): pl.pallas_call(functools.partial(layer_kernel, sizes), out_shape=jax.Shap...  120 us

profile of v7, /device:TPU:32, one launch (start us, length us, event | category | flops | bytes accessed | tf_op | source)
XLA Modules:
  0.0 121.5 jit_solution(8170733258031064637)
XLA Ops:
  0.0 119.9 %shard_map.127 = bf16[4,64,384]{2,1,0:T(8,128)(2,1)} custom-call(s32[32]{0:T(128)} %lengths_ref.1, bf16[256,1536]{1,0:T(8,128)(2,1)} %hidden_ref.1, f32[1536]{0:T(1024)} %gain_ref.1, f32[1,128]{1,0:T(1,128)} %constant.2.clone.freqs_ref, bf16[1536,384]{1,0:T(8,128)(2,1)} %w_query_ref.1, bf16[2,1536,256]{2,1,0:T(8,128)(2,1)} %w_keyval_ref.1, ...), custom_call_target="tpu_custom_call" | custom-call | tf_op jit(solution)/shard_map/pallas_call | solution.py:807
  119.9 1.6 %copy.15 = bf16[256,384]{1,0:T(8,128)(2,1)} copy(bf16[256,384]{1,0:T(8,128)(2,1)} %bitcast.3) | data formatting | bytes 393216
